TPU v7x, 32 devices: a whole 2x2x4 slice. The times are simulated.
32 devices in a mesh: wide: 4 (over y, core), sixteen: 8 (over z, x).
Axes of the slice: x: 2, y: 2, z: 4, core: 2. Of those that a mesh axis runs over, the one named last changes fastest.
Arguments:
- observations: float32 [64, 256, 512], P(None, 'sixteen', 'wide'), may hold values from -60 to 60
- huber_scale: float32 [64], replicated, may hold values from 0.5 to 2
- observed: int32 [256, 512], P('sixteen', 'wide'), may hold values from 0 to 1, as said below
- jitter: float32 [2, 256, 512], P(None, 'sixteen', 'wide'), may hold values from -0.4 to 0.4
- owner_map: int32 [4, 64], P('wide'), may hold values from 0 to 7, as said below
- neighbours: int32 [4, 64, 6], P('wide'), may hold values from 0 to 63, as said below
Outputs:
- solution: float32 [4, 8, 64, 8, 512], P('wide', 'sixteen')
- residual: float32 [4, 8, 64, 8, 512], P('wide', 'sixteen')
Inputs may be any that keep to these rules, and one draw needn't show every extreme that they name: At least one whole lattice row and at least one whole lattice column hold no observed point. `owner_map`: in each column group every device along sixteen holds 8 blocks (block g on device g // 8) and sends them to 8 different owners; every owner receives exactly 8 blocks, each from a different device. `neighbours`: block g of a column group lists g + d and g - d modulo 64 for each of half of 6 different offsets d between 1 and 4; all blocks of one group use the same offsets, so every list holds 6 different blocks and the relation is symmetric.
All inputs are finite; a program needn't handle non-finite values.
Results may differ from a plain program's by a relative error of at most 0.0003.
Values sent between devices are 32-bit elements; how exact they have to be, the bound alone decides.
A program may use at most 192 MiB of HBM per device.

v0:
```python
import functools

import jax
import jax.numpy as jnp
from jax import lax
from jax.experimental import pallas as pl
from jax.experimental.pallas import tpu as pltpu
from jax.sharding import PartitionSpec as P

BLOCK = 512
BLOCKS_DEV = 8
REACH = 4
NEIGHBOURS = 6
SWEEPS = 2

HUBER_EDGE = 1.345
NUGGET_TERM = 1.0
SILL_TERM = 0.02
ROOT_THREE = 1.7320508075688772
LOG2E = 1.4426950408889634
GROUP = 16
MESH = pl.DeviceIdType.MESH
VMEM = pl.BlockSpec(memory_space=pltpu.VMEM)
SMEM = pl.BlockSpec(memory_space=pltpu.SMEM)


def owned_table(group_map, owners, per_owner):
    total_strips = group_map.shape[0]
    member = (group_map[None, :] == jnp.arange(owners, dtype=jnp.int32)[:, None]).astype(jnp.int32)
    ranked = jnp.cumsum(member, axis=1, dtype=jnp.int32) - 1
    slot_hit = (ranked[:, :, None] == jnp.arange(per_owner, dtype=jnp.int32)[None, None, :]).astype(
        jnp.int32
    ) * member[:, :, None]
    numbers = jnp.arange(total_strips, dtype=jnp.int32)
    return jnp.sum(slot_hit * numbers[None, :, None], axis=1, dtype=jnp.int32)


def greet(sizes):
    barrier = pltpu.get_barrier_semaphore()
    for axis, n in sizes:
        me = lax.axis_index(axis)

        def say(k, carry, axis=axis, n=n, me=me):
            pl.semaphore_signal(
                barrier, inc=1, device_id={axis: lax.rem(me + k, n)}, device_id_type=MESH
            )
            return carry

        lax.fori_loop(1, n, say, 0)
    pl.semaphore_wait(barrier, sum(n - 1 for _, n in sizes))


def all_sum(buffer, axis, n, send_sem, recv_sem):
    me = lax.axis_index(axis)

    def copy(k):
        return pltpu.make_async_remote_copy(
            src_ref=buffer.at[0],
            dst_ref=buffer.at[k],
            send_sem=send_sem.at[k],
            recv_sem=recv_sem.at[k],
            device_id={axis: lax.rem(me + k, n)},
            device_id_type=MESH,
        )

    copies = [copy(k) for k in range(1, n)]
    for c in copies:
        c.start()
    for c in copies:
        c.wait()
    total = None
    for owner in range(n):
        term = buffer[lax.rem(me - owner + n, n)]
        total = term if total is None else total + term
    return total


def swap(x):
    return pltpu.roll(x, x.shape[-1] // 2, x.ndim - 1)


def fold(x):
    return x + swap(x)


def halves(x, fields):
    return lax.broadcasted_iota(jnp.int32, x.shape, x.ndim - 1) < fields


def halo_copies(halo, rows, reach, n, send_sem, recv_sem, axis="sixteen"):
    me = lax.axis_index(axis)
    up, down = lax.rem(me + 1, n), lax.rem(me + n - 1, n)
    return [
        pltpu.make_async_remote_copy(
            src_ref=halo.at[pl.ds(rows, reach)],
            dst_ref=halo.at[pl.ds(0, reach)],
            send_sem=send_sem.at[0],
            recv_sem=recv_sem.at[0],
            device_id={axis: up},
            device_id_type=MESH,
        ),
        pltpu.make_async_remote_copy(
            src_ref=halo.at[pl.ds(reach, reach)],
            dst_ref=halo.at[pl.ds(reach + rows, reach)],
            send_sem=send_sem.at[1],
            recv_sem=recv_sem.at[1],
            device_id={axis: down},
            device_id_type=MESH,
        ),
    ]


def edge_copies(source, target, reach, n, send_sem, recv_sem):
    me = lax.axis_index("sixteen")
    rows = source.shape[0]
    return [
        pltpu.make_async_remote_copy(
            src_ref=source.at[pl.ds(first, reach)],
            dst_ref=target.at[pl.ds(side * reach, reach)],
            send_sem=send_sem.at[side],
            recv_sem=recv_sem.at[side],
            device_id={"sixteen": lax.rem(me + shift, n)},
            device_id_type=MESH,
        )
        for side, first, shift in ((0, rows - reach, 1), (1, 0, n - 1))
    ]


def polish_kernel(
    nw, ns, fields, reach,
    obs, weight, scale, place, halo, place_halo,
    row_eff, row_cnt, col_eff, col_cnt, obs_edge, row_edge,
    row_buf0, row_buf1, col_buf0, col_buf1,
    sems_s, sems_r,
):
    rows, cols, lanes = obs.shape
    half = cols // 2
    place_rows = place.shape[0]
    place_reach = 2 * reach
    greet((("wide", nw), ("sixteen", ns)))
    place_halo[pl.ds(place_reach, place_rows)] = place[...]
    place_copies = halo_copies(
        place_halo, place_rows, place_reach, ns, sems_s.at[6], sems_r.at[6]
    )
    obs_copies = edge_copies(obs, obs_edge, reach, ns, sems_s.at[7], sems_r.at[7])
    row_copies = edge_copies(row_eff, row_edge, reach, ns, sems_s.at[8], sems_r.at[8])
    for c in place_copies + obs_copies:
        c.start()
    edge = HUBER_EDGE
    diagonal = lax.broadcasted_iota(jnp.int32, (cols, lanes), 0) == lax.broadcasted_iota(
        jnp.int32, (cols, lanes), 1
    )
    inv = 1.0 / scale[...]
    row_eff[...] = jnp.zeros_like(row_eff)
    col_eff[...] = jnp.zeros_like(col_eff)
    for sweep in range(SWEEPS):
        row_buf = (row_buf0, row_buf1)[min(sweep, 1)]
        col_buf = (col_buf0, col_buf1)[min(sweep, 1)]

        def clipped(r):
            value = (obs[r] - row_eff[pl.ds(r, 1)] - col_eff[...]) * inv
            return weight[r] * jnp.clip(value, -edge, edge)

        def row_step(r, carry):
            row_buf[0, pl.ds(r, 1)] = jnp.sum(clipped(r), axis=0, keepdims=True)
            if sweep == 0:
                row_buf[0, pl.ds(rows + r, 1)] = jnp.sum(weight[r], axis=0, keepdims=True)
            return carry

        lax.fori_loop(0, rows, row_step, 0)
        total = all_sum(row_buf, "wide", nw, sems_s.at[sweep], sems_r.at[sweep])
        if sweep == 0:
            row_cnt[...] = jnp.maximum(total[rows:], 1.0)
        row_eff[...] = row_eff[...] + scale[...] * total[:rows] / row_cnt[...]
        if sweep == SWEEPS - 1:
            for c in row_copies:
                c.start()

        def col_step(r, carry):
            return carry + clipped(r)

        part = lax.fori_loop(0, rows, col_step, jnp.zeros((cols, lanes), jnp.float32))

        def packed(x):
            x = fold(x)
            low, high = x[:half], x[half:]
            return jnp.where(halves(low, fields), low, high)

        def unpacked(y):
            z = swap(y)
            first = halves(y, fields)
            return jnp.concatenate([jnp.where(first, y, z), jnp.where(first, z, y)], axis=0)

        col_buf[0, pl.ds(0, half)] = packed(part)
        if sweep == 0:
            col_buf[0, pl.ds(half, 8)] = jnp.zeros((8, lanes), jnp.float32)
            count = lax.fori_loop(
                0, rows, lambda r, c: c + weight[r], jnp.zeros((cols, lanes), jnp.float32)
            )
            col_buf[0, pl.ds(half, 1)] = jnp.sum(
                jnp.where(diagonal, fold(count), 0.0), axis=0, keepdims=True
            )
        total = all_sum(col_buf, "sixteen", ns, sems_s.at[2 + sweep], sems_r.at[2 + sweep])
        if sweep == 0:
            spread = jnp.where(diagonal, jnp.broadcast_to(total[half : half + 1], (cols, lanes)), 0.0)
            count = jnp.sum(spread, axis=1, keepdims=True)
            col_cnt[...] = jnp.maximum(jnp.broadcast_to(count, (cols, lanes)), 1.0)
        col_eff[...] = col_eff[...] + scale[...] * unpacked(total[:half]) / col_cnt[...]

    def rest(r, carry):
        value = weight[r] * (obs[r] - row_eff[pl.ds(r, 1)] - col_eff[...])
        halo[reach + r] = value
        return carry

    lax.fori_loop(0, rows, rest, 0)
    for c in place_copies + row_copies + obs_copies:
        c.wait()

    def across(row):
        spread = jnp.where(diagonal, jnp.broadcast_to(row, (cols, lanes)), 0.0)
        return jnp.broadcast_to(jnp.sum(spread, axis=1, keepdims=True), (cols, lanes))

    def beside(first):
        def one(q, carry):
            t = first + q
            even = across(place_halo[2 * t, 2:3])
            odd = across(place_halo[2 * t + 1, 2:3])
            seen = jnp.where(halves(even, fields), even, odd)
            at = q if first == 0 else reach + q
            halo[t] = seen * (obs_edge[at] - row_edge[pl.ds(at, 1)] - col_eff[...])
            return carry

        lax.fori_loop(0, reach, one, 0)

    beside(0)
    beside(reach + rows)


def middle_kernel(ns, reach, row_map, halo_in, image, alpha, beta, halo, send_sem, recv_sem):
    greet((("sixteen", ns),))

    def direct(r, carry):
        before = halo_in[reach + r]
        halo[reach + r] = (before - alpha[...] * image[row_map[r]]) + beta[...] * before
        return carry

    lax.fori_loop(0, image.shape[0], direct, 0)
    copies = halo_copies(halo, image.shape[0], reach, ns, send_sem, recv_sem)
    for c in copies:
        c.start()
    for c in copies:
        c.wait()


def build_windows(halo, windows, starts, span, fields, strip_rows):
    blocks = windows.shape[1]
    pairs = strip_rows // 2

    def one(h, carry):
        for pair in range(pairs):
            for i, start in enumerate(starts):
                x = halo[h * pairs + pair, start : start + span, :]
                first = halves(x, fields)
                z = swap(x)
                for parity in range(2):
                    y = jnp.where(first, x, z) if parity == 0 else jnp.where(first, z, x)
                    high = y.astype(jnp.bfloat16).astype(jnp.float32)
                    both = jnp.where(first, high, y - high).astype(jnp.bfloat16)
                    at = (2 * pair + parity) * span
                    windows[i, h, at : at + span, :] = both
        return carry

    lax.fori_loop(0, blocks, one, 0)


def finish(i, acc, own_of, store, dots, fields, strip_rows):
    rows = strip_rows * GROUP
    y = fold(acc[:rows] + acc[rows:])
    at = pl.multiple_of(i * GROUP, GROUP)
    for pair in range(strip_rows // 2):
        even = y[(2 * pair) * GROUP : (2 * pair + 1) * GROUP]
        odd = y[(2 * pair + 1) * GROUP : (2 * pair + 2) * GROUP]
        own = own_of(pair, at)
        value = NUGGET_TERM * own + jnp.where(halves(even, fields), even, odd)
        store(pair, at, value)
        dots[0:1] += jnp.sum(own * value, axis=0, keepdims=True)
        dots[1:2] += jnp.sum(value * value, axis=0, keepdims=True)
        dots[2:3] += jnp.sum(own * own, axis=0, keepdims=True)


def shifted(staged, received, n, send_sem, recv_sem):
    me = lax.axis_index("sixteen")
    return [pltpu.make_async_copy(staged.at[0], received.at[0], send_sem.at[0])] + [
        pltpu.make_async_remote_copy(
            src_ref=staged.at[k],
            dst_ref=received.at[k],
            send_sem=send_sem.at[k],
            recv_sem=recv_sem.at[k],
            device_id={"sixteen": lax.rem(me + k, n)},
            device_id_type=MESH,
        )
        for k in range(1, n)
    ]


def stage(staged, source, first, chosen):
    slots, pairs = staged.shape[:2]

    def one(k, carry):
        for pair in range(pairs):
            staged[k, pair] = source[first + chosen[k] * pairs + pair]
        return carry

    lax.fori_loop(0, slots, one, 0)


def keep(staged_image, local_image, slot, pairs, pair, at, value):
    if staged_image.shape[0] == BLOCKS_DEV:
        staged_image[slot, pair, pl.ds(at, GROUP), :] = value
    else:
        local_image[slot * pairs + pair, pl.ds(at, GROUP), :] = value


def slot_of(ns, g):
    return lax.rem(g + 1, BLOCKS_DEV) if ns == BLOCKS_DEV else g


def send_image(ns, g, images, staged_image, local_image, chosen):
    if ns == BLOCKS_DEV:
        for k in range(ns):

            @pl.when(g == (k - 1) % ns)
            def _(k=k):
                images[k].start()

    else:

        @pl.when(g == BLOCKS_DEV - 1)
        def _():
            stage(staged_image, local_image, 0, chosen)
            for c in images:
                c.start()


def first_image_kernel(
    nw, ns, starts, span, reach, fields, strip_rows,
    offs, step_block, chosen, halo, others, centre,
    tiles, image, alpha, beta, norm_next, received, received_image,
    windows, dots, staged, staged_image, local_image, dot_w, dot_s,
    send_sem, recv_sem, send_image_sem, recv_image_sem, sems_s, sems_r,
):
    g = pl.program_id(0)
    slot = slot_of(ns, g)
    pairs = strip_rows // 2
    spread = 2.0 * strip_rows
    cutoff = 6.0 * strip_rows
    wide = strip_rows * span
    rows = strip_rows * GROUP

    @pl.when(g == 0)
    def _():
        stage(staged, halo, reach, chosen)
        greet((("wide", nw), ("sixteen", ns)))
        for c in shifted(staged, received, ns, send_sem, recv_sem):
            c.start()
        build_windows(halo, windows, starts, span, fields, strip_rows)
        dots[...] = jnp.zeros_like(dots)

    block = step_block[g]

    def one(i, carry):
        here = centre[block, i]
        row_here = jnp.broadcast_to(here[:, 0:1], (rows, wide))
        col_here = jnp.broadcast_to(here[:, 1:2], (rows, wide))
        acc = jnp.zeros((2 * rows, 2 * fields), jnp.float32)
        for n in range(NEIGHBOURS + 1):
            h = block + REACH + offs[n]
            pair = others[h, i]
            row_gap = pair[0:1] - row_here
            col_gap = pair[1:2] - col_here
            square = row_gap * row_gap + col_gap * col_gap
            distance = square * lax.rsqrt(jnp.maximum(square, 1e-30))
            fading = jnp.maximum(1.0 - distance * (1.0 / cutoff), 0.0)
            fading = fading * fading
            fading = fading * fading
            decay = jnp.exp2(distance * (-ROOT_THREE * LOG2E / spread))
            weight = SILL_TERM * (NEIGHBOURS + 1.0 if n == 0 else 1.0)
            lead = weight * (ROOT_THREE / spread) * distance + weight
            kernel = lead * decay * fading * (1.0 + distance * (4.0 / cutoff))
            high = kernel.astype(jnp.bfloat16)
            low = (kernel - high.astype(jnp.float32)).astype(jnp.bfloat16)
            both = jnp.concatenate([high, low], axis=0)
            tiles[0, i, :, n * wide : (n + 1) * wide] = both
            acc = acc + jnp.dot(both, windows[i, h], preferred_element_type=jnp.float32)

        def store(pair, at, value):
            image[pair, pl.ds(at, GROUP), :] = value
            keep(staged_image, local_image, slot, pairs, pair, at, value)

        def own_of(pair, at):
            return halo[reach + block * pairs + pair, pl.ds(at, GROUP), :]

        finish(i, acc, own_of, store, dots, fields, strip_rows)
        return carry

    lax.fori_loop(0, len(starts), one, 0)
    images = shifted(staged_image, received_image, ns, send_image_sem, recv_image_sem)
    send_image(ns, g, images, staged_image, local_image, chosen)

    @pl.when(g == pl.num_programs(0) - 1)
    def _():
        dot_w[0] = fold(dots[...])
        dot_s[0] = all_sum(dot_w, "wide", nw, sems_s.at[0], sems_r.at[0])
        total = all_sum(dot_s, "sixteen", ns, sems_s.at[1], sems_r.at[1])
        norm = total[2:3]
        step = norm / total[0:1]
        after = (norm - 2.0 * step * total[0:1]) + step * step * total[1:2]
        alpha[...] = step
        beta[...] = after / norm
        norm_next[...] = after
        for c in shifted(staged, received, ns, send_sem, recv_sem):
            c.wait()
        for c in images:
            c.wait()


def second_image_kernel(
    nw, ns, starts, span, reach, fields, strip_rows,
    offs, step_block, chosen, halo, norm, tiles,
    alpha, received_image,
    windows, dots, staged_image, local_image, dot_w, dot_s,
    send_image_sem, recv_image_sem, sems_s, sems_r,
):
    g = pl.program_id(0)
    last = pl.num_programs(0) - 1
    pairs = strip_rows // 2
    wide = strip_rows * span
    rows = strip_rows * GROUP
    slot = slot_of(ns, g)

    @pl.when(g == 0)
    def _():
        greet((("wide", nw), ("sixteen", ns)))
        build_windows(halo, windows, starts, span, fields, strip_rows)
        dots[...] = jnp.zeros_like(dots)

    block = step_block[g]

    def one(i, carry):
        acc = jnp.zeros((2 * rows, 2 * fields), jnp.float32)
        for n in range(NEIGHBOURS + 1):
            h = block + REACH + offs[n]
            acc = acc + jnp.dot(
                tiles[0, i, :, n * wide : (n + 1) * wide],
                windows[i, h],
                preferred_element_type=jnp.float32,
            )

        def store(pair, at, value):
            keep(staged_image, local_image, slot, pairs, pair, at, value)

        def own_of(pair, at):
            return halo[reach + block * pairs + pair, pl.ds(at, GROUP), :]

        finish(i, acc, own_of, store, dots, fields, strip_rows)
        return carry

    lax.fori_loop(0, len(starts), one, 0)
    images = shifted(staged_image, received_image, ns, send_image_sem, recv_image_sem)
    send_image(ns, g, images, staged_image, local_image, chosen)

    @pl.when(g == last)
    def _():
        dot_w[0] = fold(dots[...])
        dot_s[0] = all_sum(dot_w, "wide", nw, sems_s.at[0], sems_r.at[0])
        total = all_sum(dot_s, "sixteen", ns, sems_s.at[1], sems_r.at[1])
        alpha[...] = norm[...] / total[0:1]
        for c in images:
            c.wait()


def final_kernel(fields, strip_rows, came, start, middle, image, alpha0, alpha1, beta, out, rest):
    pairs, cols = start.shape[1:3]
    lead = alpha0[...] + alpha1[...] * beta[...]
    step = alpha1[...]
    for j in range(BLOCKS_DEV):
        k = came[j]
        for pair in range(pairs):
            first = start[k, pair]
            value = first - alpha0[...] * middle[k, pair]
            first = (lead * first + step * value).T
            second = (value - step * image[k, pair]).T
            for parity in range(2):
                at = (2 * pair + parity) * cols
                part = slice(parity * fields, (parity + 1) * fields)
                out[:, j, at : at + cols] = first[part]
                rest[:, j, at : at + cols] = second[part]


def on_device(observations, huber_scale, observed, jitter, owner_map, neighbours):
    fields, row_dev, col_dev = observations.shape
    nw, ns = lax.axis_size("wide"), lax.axis_size("sixteen")
    my_place = lax.axis_index("sixteen")
    group_place = lax.axis_index("wide")
    strip_rows = BLOCK // col_dev
    total_strips = BLOCKS_DEV * ns
    rows, lanes = row_dev // 2, 2 * fields
    pairs = strip_rows // 2
    reach = REACH * pairs
    f32 = jnp.float32
    shape = jax.ShapeDtypeStruct

    def pack(x):
        return x.reshape(fields, rows, 2, col_dev).transpose(1, 3, 2, 0).reshape(rows, col_dev, lanes)

    obs = pack(observations)
    weight = pack(jnp.broadcast_to(observed.astype(f32)[None], observations.shape))
    scale = jnp.concatenate([huber_scale, huber_scale])[None]
    row_place = (my_place * row_dev + jnp.arange(row_dev, dtype=jnp.int32)).astype(f32)
    col_place = (group_place * col_dev + jnp.arange(col_dev, dtype=jnp.int32)).astype(f32)
    place = jnp.stack(
        [row_place[:, None] + jitter[0], col_place[None, :] + jitter[1], observed.astype(f32)],
        axis=1,
    )
    most = max(nw, ns)
    halo, place_halo = pl.pallas_call(
        functools.partial(polish_kernel, nw, ns, fields, reach),
        out_shape=(
            shape((rows + 2 * reach, col_dev, lanes), f32),
            shape((row_dev + 4 * reach, 3, col_dev), f32),
        ),
        in_specs=[VMEM] * 4,
        out_specs=(VMEM,) * 2,
        scratch_shapes=[
            pltpu.VMEM((rows, lanes), f32),
            pltpu.VMEM((rows, lanes), f32),
            pltpu.VMEM((col_dev, lanes), f32),
            pltpu.VMEM((col_dev, lanes), f32),
            pltpu.VMEM((2 * reach, col_dev, lanes), f32),
            pltpu.VMEM((2 * reach, lanes), f32),
            pltpu.VMEM((nw, 2 * rows, lanes), f32),
            pltpu.VMEM((nw, rows, lanes), f32),
            pltpu.VMEM((ns, col_dev // 2 + 8, lanes), f32),
            pltpu.VMEM((ns, col_dev // 2, lanes), f32),
            pltpu.SemaphoreType.DMA((9, most)),
            pltpu.SemaphoreType.DMA((9, most)),
        ],
        compiler_params=pltpu.CompilerParams(collective_id=0, has_side_effects=True),
    )(obs, weight, scale, place)

    cut = 6 * strip_rows
    span = GROUP + 2 * cut
    starts = tuple(
        min(max(GROUP * i - cut, 0), col_dev - span) for i in range(col_dev // GROUP)
    )
    groups = len(starts)
    wide = strip_rows * span
    blocks_halo = BLOCKS_DEV + 2 * REACH
    by_block = place_halo[:, :2].reshape(blocks_halo, strip_rows, 2, col_dev)
    others = jnp.stack([by_block[..., s : s + span] for s in starts], axis=1)
    others = others.transpose(0, 1, 3, 2, 4).reshape(blocks_halo, groups, 2, wide)
    centre = place[:, :2].reshape(BLOCKS_DEV, strip_rows, 2, groups, GROUP)
    centre = centre.transpose(0, 3, 1, 4, 2).reshape(BLOCKS_DEV, groups, strip_rows * GROUP, 2)
    listed = (neighbours[0, 0] + total_strips // 2) % total_strips - total_strips // 2
    offs = jnp.concatenate([jnp.zeros((1,), jnp.int32), listed])

    tile_block = (1, groups, 2 * strip_rows * GROUP, (NEIGHBOURS + 1) * wide)
    tile_shape = shape((BLOCKS_DEV,) + tile_block[1:], jnp.bfloat16)
    whole_halo = pl.BlockSpec((rows + 2 * reach, col_dev, lanes), lambda g: (0, 0, 0))
    tile_spec = pl.BlockSpec(tile_block, lambda g: (g, 0, 0, 0))
    image_spec = pl.BlockSpec((pairs, col_dev, lanes), lambda g: (g, 0, 0))
    dots_spec = pl.BlockSpec((1, lanes), lambda g: (0, 0))
    image_shape = shape((rows, col_dev, lanes), f32)
    dots_shape = shape((1, lanes), f32)
    window_scratch = pltpu.VMEM((groups, blocks_halo, wide, lanes), jnp.bfloat16)
    static = (starts, span, reach, fields, strip_rows)
    group_map = owner_map[0]
    numbers = jnp.arange(BLOCKS_DEV, dtype=jnp.int32)
    table = owned_table(group_map, ns, BLOCKS_DEV)
    my_ids = lax.dynamic_index_in_dim(table, my_place, 0, keepdims=False)
    my_targets = lax.dynamic_slice_in_dim(group_map, my_place * BLOCKS_DEV, BLOCKS_DEV)
    owners = (my_place + jnp.arange(ns, dtype=jnp.int32)) % ns
    hit = my_targets[None, :] == owners[:, None]
    chosen = jnp.sum(hit * numbers[None], axis=1, dtype=jnp.int32)
    came = (my_place - my_ids // BLOCKS_DEV + ns) % ns
    if ns == BLOCKS_DEV:
        step_block = jnp.roll(chosen, -1)
        step_of = jnp.sum(
            (step_block[None, :] == numbers[:, None]) * numbers[None], axis=1, dtype=jnp.int32
        )
    else:
        step_block = step_of = numbers
    row_map = (step_of[:, None] * pairs + jnp.arange(pairs, dtype=jnp.int32)[None]).reshape(-1)
    anywhere = pl.BlockSpec(memory_space=pl.ANY)
    moved_shape = shape((ns, pairs, col_dev, lanes), f32)
    staging = pltpu.VMEM(moved_shape.shape, f32)

    sum_scratch = [
        pltpu.VMEM((3, lanes), f32),
        pltpu.VMEM((nw, 3, lanes), f32),
        pltpu.VMEM((ns, 3, lanes), f32),
    ]
    local = pltpu.VMEM((8, 128) if ns == BLOCKS_DEV else (rows, col_dev, lanes), f32)
    tiles, image, alpha0, beta, norm1, start, first_image = pl.pallas_call(
        functools.partial(first_image_kernel, nw, ns, *static),
        grid=(BLOCKS_DEV,),
        out_shape=(tile_shape, image_shape) + (dots_shape,) * 3 + (moved_shape,) * 2,
        in_specs=[
            SMEM,
            SMEM,
            SMEM,
            whole_halo,
            pl.BlockSpec((blocks_halo, groups, 2, wide), lambda g: (0, 0, 0, 0)),
            pl.BlockSpec((BLOCKS_DEV, groups, strip_rows * GROUP, 2), lambda g: (0, 0, 0, 0)),
        ],
        out_specs=(tile_spec, image_spec) + (dots_spec,) * 3 + (anywhere,) * 2,
        scratch_shapes=[window_scratch, sum_scratch[0], staging, staging, local]
        + sum_scratch[1:]
        + [pltpu.SemaphoreType.DMA((ns,))] * 4
        + [pltpu.SemaphoreType.DMA((2, most))] * 2,
        compiler_params=pltpu.CompilerParams(collective_id=3, has_side_effects=True),
    )(offs, step_block, chosen, halo, others, centre)

    halo1 = pl.pallas_call(
        functools.partial(middle_kernel, ns, reach),
        out_shape=shape(halo.shape, f32),
        in_specs=[SMEM] + [VMEM] * 4,
        out_specs=VMEM,
        scratch_shapes=[pltpu.SemaphoreType.DMA((2,))] * 2,
        compiler_params=pltpu.CompilerParams(collective_id=1, has_side_effects=True),
    )(row_map, halo, image, alpha0, beta)
    alpha1, last_image = pl.pallas_call(
        functools.partial(second_image_kernel, nw, ns, *static),
        grid=(BLOCKS_DEV,),
        out_shape=(dots_shape, moved_shape),
        in_specs=[SMEM, SMEM, SMEM, whole_halo, dots_spec, tile_spec],
        out_specs=(dots_spec, anywhere),
        scratch_shapes=[window_scratch, sum_scratch[0], staging, local]
        + sum_scratch[1:]
        + [pltpu.SemaphoreType.DMA((ns,))] * 2
        + [pltpu.SemaphoreType.DMA((2, most))] * 2,
        compiler_params=pltpu.CompilerParams(collective_id=2, has_side_effects=True),
    )(offs, step_block, chosen, halo1, norm1, tiles)

    out_shape = shape((fields, BLOCKS_DEV, BLOCK), f32)
    solution_now, residual_now = pl.pallas_call(
        functools.partial(final_kernel, fields, strip_rows),
        out_shape=(out_shape, out_shape),
        in_specs=[SMEM] + [VMEM] * 6,
        out_specs=(VMEM, VMEM),
    )(came, start, first_image, last_image, alpha0, alpha1, beta)
    return solution_now[None, None], residual_now[None, None]


def solution(mesh):
    return jax.shard_map(
        on_device,
        mesh=mesh,
        in_specs=(
            P(None, "sixteen", "wide"),
            P(),
            P("sixteen", "wide"),
            P(None, "sixteen", "wide"),
            P("wide", None),
            P("wide", None, None),
        ),
        out_specs=(P("wide", "sixteen", None, None, None), P("wide", "sixteen", None, None, None)),
        check_vma=False,
    )
```

profile of v0, /device:TPU:10, one launch (start us, length us, event | category | flops | bytes accessed | tf_op | source)
XLA Modules:
  0.0 208.3 jit_solution(3946959562940326392)
XLA Ops:
  0.6 0.7 fusion.8
  1.3 0.2 reduce_window_sum.11
  1.5 0.2 multiply_reduce_fusion
  1.7 0.6 and_select_fusion
  2.3 0.9 add_reduce_fusion
  3.2 0.6 pad_add_fusion.offs
  3.8 0.7 dynamic-slice_bitcast_fusion
  4.5 0.2 select_reduce_fusion.1.chosen
  4.7 0.0 copy-start.2
  4.7 0.1 slice.43
  4.8 0.7 pad_add_fusion.1.step_block
  5.4 0.0 copy-start.1
  5.4 1.8 copy.41
  7.3 1.3 copy.42.obs
  8.6 0.0 copy-done.2
  8.6 0.0 copy-done.1
  8.6 0.0 copy-start.4
  8.6 0.0 copy-start
  8.6 0.1 broadcast_in_dim.11
  8.7 1.3 copy.43.weight
  10.0 0.0 copy-done.4
  10.0 0.7 maximum_bitcast_fusion.1.scale
  10.7 0.0 copy-done
  10.7 0.1 broadcast_add_fusion
  10.8 0.7 pad_maximum_fusion.place
  11.5 48.9 %shard_map.77 = (f32[32,128,128]{2,1,0:T(8,128)}, f32[64,3,128]{2,1,0:T(4,128)}) custom-call(f32[16,128,128]{2,1,0:T(8,128)} %copy.42.obs, f32[16,128,128]{2,1,0:T(8,128)} %copy.43.weight, f32[1,128]{1,0:T(1,128)} %maximum_bitcast_fusion.1.scale, f32[32,3,128]{2,1,0:T(4,128)} %pad_maximum_fusion.place), custom_call_target="tpu_custom_call" | custom-call | tf_op jit(solution)/shard_map/pallas_call | solution.py:526
  60.4 0.9 slice.47
  61.4 0.4 fusion.13
  62.0 1.1 reshape.198.others
  63.1 0.1 squeeze.20
  63.2 0.1 squeeze.19
  63.3 0.1 bitcast_add_fusion
  63.5 2.9 %copy.52 = f32[8,8,4,16,2]{4,3,2,1,0:T(8,128)} copy(f32[8,8,4,16,2]{3,1,4,2,0:T(8,128)S(1)} %maximum_bitcast_fusion) | data formatting | bytes 65536 | tf_op jit(solution)/shard_map/transpose | solution.py:563
  66.4 0.0 copy-start.3
  66.4 63.8 %shard_map.78 = (bf16[8,8,128,1792]{3,2,1,0:T(8,128)(2,1)}, f32[16,128,128]{2,1,0:T(8,128)}, f32[1,128]{1,0:T(1,128)}, f32[1,128]{1,0:T(1,128)}, f32[1,128]{1,0:...) custom-call(s32[7]{0:T(128)} %pad_add_fusion.offs, s32[8]{0:T(128)} %pad_add_fusion.1.step_block, ...), custom_call_target="tpu_custom_call" | custom-call | tf_op jit(solution)/shard_map/pallas_call | solution.py:604
  130.2 0.0 copy-done.3
  130.2 0.1 select_reduce_fusion
  130.3 0.1 iota_add_fusion
  130.4 0.6 add.176.row_map
  131.0 29.7 %shard_map.79.halo = f32[32,128,128]{2,1,0:T(8,128)} custom-call(s32[16]{0:T(128)} %add.176.row_map, f32[32,128,128]{2,1,0:T(8,128)} %get-tuple-element.15.halo.halo_in, f32[16,128,128]{2,1,0:T(8,128)} %get-tuple-element.19.image, f32[1,128]{1,0:T(1,128)} %get-tuple-element.20.alpha.alpha0, f32[1,128]{1,0:T(1,128)} %get-tuple-element.21.beta), custom_call_target="tpu_custom_call" | custom-call | tf_op jit(solution)/shard_map/pallas_call | solution.py:624
  160.7 42.1 %shard_map.80 = (f32[1,128]{1,0:T(1,128)}, f32[8,2,128,128]{3,2,1,0:T(8,128)}) custom-call(s32[7]{0:T(128)} %pad_add_fusion.offs, s32[8]{0:T(128)} %pad_add_fusion.1.step_block, s32[8]{0:T(128)} %copy-done.2, f32[32,128,128]{2,1,0:T(8,128)} %shard_map.79.halo, f32[1,128]{1,0:T(1,128)} %get-tuple-element.22.norm, ...), custom_call_target="tpu_custom_call" | custom-call | tf_op jit(solution)/shard_map/pallas_call | solution.py:632
  202.8 5.6 %shard_map.81 = (f32[64,8,512]{2,1,0:T(8,128)}, f32[64,8,512]{2,1,0:T(8,128)}) custom-call(s32[8]{0:T(128)} %get-tuple-element.37.came, f32[8,2,128,128]{3,2,1,0:T(8,128)} %get-tuple-element.17.start, f32[8,2,128,128]{3,2,1,0:T(8,128)} %get-tuple-element.18.middle, f32[8,2,128,128]{3,2,1,0:T(8,128)} %get-tuple-element.24.image, ...), custom_call_target="tpu_custom_call" | custom-call | tf_op jit(solution)/shard_map/pallas_call | solution.py:646
  (18 shorter events, 0.3 us)
Async XLA Ops:
  4.7 3.9 %copy-start.2 = (s32[8]{0:T(128)}, s32[8]{0:T(128)S(1)}, u32[]{:S(2)}) copy-start(s32[8]{0:T(128)S(1)} %select_reduce_fusion.1.chosen) | copy-start | bytes 100
  5.4 3.2 %copy-start.1 = (s32[32,128]{1,0:T(8,128)S(1)}, s32[32,128]{1,0:T(8,128)}, u32[]{:S(2)}) copy-start(s32[32,128]{1,0:T(8,128)} %param.8) | copy-start | bytes 49156
  8.6 1.4 copy-start.4
  8.6 2.1 copy-start
  66.4 63.8 %copy-start.3 = (s32[8]{0:T(128)S(1)}, s32[8]{0:T(128)}, u32[]{:S(2)}) copy-start(s32[8]{0:T(128)} %pad_add_fusion.1.step_block) | copy-start | bytes 100
where the time goes:
time: 211 us; the launch traced here: 208 us
  Pallas kernels  190 us (90%)
  local copies, waits for them, and re-layouts  11.7 us (6%)
  other arithmetic  5.77 us (3%)
    pallas_call x1, Pallas kernels, on_device(): pl.pallas_call(functools.partial(first_image_kernel, nw, ns, *static), gr...  63.8 us
    pallas_call x1, Pallas kernels, on_device(): pl.pallas_call(functools.partial(polish_kernel, nw, ns, fields, reach), o...  48.9 us
    pallas_call x1, Pallas kernels, on_device(): pl.pallas_call(functools.partial(second_image_kernel, nw, ns, *static), g...  42.1 us
    pallas_call x1, Pallas kernels, on_device(): pl.pallas_call(functools.partial(middle_kernel, ns, reach), out_shape=sha...  29.7 us
    pallas_call x1, Pallas kernels, on_device(): pl.pallas_call(functools.partial(final_kernel, fields, strip_rows), out_s...  5.56 us

commit v1 on v0

v1 whole, which is shorter than its diff:
```python
import functools

import jax
import jax.numpy as jnp
from jax import lax
from jax.experimental import pallas as pl
from jax.experimental.pallas import tpu as pltpu
from jax.sharding import PartitionSpec as P

BLOCK = 512
BLOCKS_DEV = 8
REACH = 4
NEIGHBOURS = 6
SWEEPS = 2

HUBER_EDGE = 1.345
NUGGET_TERM = 1.0
SILL_TERM = 0.02
ROOT_THREE = 1.7320508075688772
LOG2E = 1.4426950408889634
GROUP = 16
MESH = pl.DeviceIdType.MESH
VMEM = pl.BlockSpec(memory_space=pltpu.VMEM)
SMEM = pl.BlockSpec(memory_space=pltpu.SMEM)
F32 = jnp.float32


def say_hello(sizes):
    barrier = pltpu.get_barrier_semaphore()
    for axis, n in sizes:
        me = lax.axis_index(axis)

        def say(k, carry, axis=axis, n=n, me=me):
            pl.semaphore_signal(
                barrier, inc=1, device_id={axis: lax.rem(me + k, n)}, device_id_type=MESH
            )
            return carry

        lax.fori_loop(1, n, say, 0)


def hear_hello(sizes):
    pl.semaphore_wait(pltpu.get_barrier_semaphore(), sum(n - 1 for _, n in sizes))


def remote(src, dst, send, recv, axis, n, shift):
    return pltpu.make_async_remote_copy(
        src_ref=src,
        dst_ref=dst,
        send_sem=send,
        recv_sem=recv,
        device_id={axis: lax.rem(lax.axis_index(axis) + shift, n)},
        device_id_type=MESH,
    )


def start(copies):
    for c in copies:
        c.start()


def wait(copies):
    for c in copies:
        c.wait()


def spread_copies(buffer, axis, n, send, recv):
    return [
        remote(buffer.at[0], buffer.at[k], send.at[k], recv.at[k], axis, n, k) for k in range(1, n)
    ]


def gathered_sum(buffer, axis, n):
    me = lax.axis_index(axis)
    total = None
    for owner in range(n):
        term = buffer[lax.rem(me - owner + n, n)]
        total = term if total is None else total + term
    return total


def exchange_copies(staged, received, n, send, recv):
    return [pltpu.make_async_copy(staged.at[0], received.at[0], send.at[0])] + [
        remote(staged.at[k], received.at[k], send.at[k], recv.at[k], "sixteen", n, k)
        for k in range(1, n)
    ]


def edge_copies(source, target, reach, n, send, recv):
    rows = source.shape[0]
    return [
        remote(
            source.at[pl.ds(first, reach)],
            target.at[pl.ds(side * reach, reach)],
            send.at[side],
            recv.at[side],
            "sixteen",
            n,
            shift,
        )
        for side, first, shift in ((0, rows - reach, 1), (1, 0, n - 1))
    ]


def swap(x):
    return pltpu.roll(x, x.shape[-1] // 2, x.ndim - 1)


def fold(x):
    return x + swap(x)


def low_lanes(x):
    return lax.broadcasted_iota(jnp.int32, x.shape, x.ndim - 1) < x.shape[-1] // 2


def beside(even, odd):
    return jnp.where(low_lanes(even), even, odd)


def turned(x, size):
    rows = x.shape[0]
    if rows < size:
        x = jnp.concatenate([x, jnp.zeros((size - rows, x.shape[1]), x.dtype)], axis=0)
    return x.T


def across(x, k, shape):
    return jnp.broadcast_to(x[:, k : k + 1], shape)


def solve_kernel(
    nw, ns, fields, strip_rows, starts, span, static_came,
    owner, listed, came, obs_in, scale_in, seen_in, jitter_in,
    out, rest,
    offs, chosen,
    obs, weight, edge, q, q_edge, staged_p, recv_p, staged_q, recv_q, staged_w, recv_w,
    tiles, win, cb, oth, place, coords,
    scale, row_eff, row_cnt, col_eff, col_cnt, row_edge, row_buf0, row_buf1, col_buf0, col_buf1,
    dots, dot_w, dot_s,
    sem_s, sem_r, exch_s, exch_r, halo_s, halo_r,
):
    rows, cols, lanes = obs.shape
    half = cols // 2
    pairs = strip_rows // 2
    reach = REACH * pairs
    row_dev = 2 * rows
    row_reach = 2 * reach
    groups = len(starts)
    wide = strip_rows * span
    tile_rows = strip_rows * GROUP
    total_strips = BLOCKS_DEV * ns
    me = lax.axis_index("sixteen")
    group_me = lax.axis_index("wide")
    everyone = (("wide", nw), ("sixteen", ns))
    full = (cols, lanes)

    say_hello(everyone)

    def pack(r, carry):
        both = jnp.concatenate(
            [obs_in[pl.ds(2 * r + parity, fields, stride=row_dev), :] for parity in range(2)],
            axis=0,
        )
        obs[r] = both.T
        return carry

    lax.fori_loop(0, rows, pack, 0)

    row_number = lax.broadcasted_iota(jnp.int32, (row_dev, cols), 0) + me * row_dev
    col_number = lax.broadcasted_iota(jnp.int32, (row_dev, cols), 1) + group_me * cols
    seen = seen_in[...].astype(F32)
    place[0, pl.ds(row_reach, row_dev)] = row_number.astype(F32) + jitter_in[0]
    place[1, pl.ds(row_reach, row_dev)] = col_number.astype(F32) + jitter_in[1]
    place[2, pl.ds(row_reach, row_dev)] = seen

    for n in range(NEIGHBOURS):
        other = listed[n, 0]
        offs[n + 1] = jnp.where(other < total_strips // 2, other, other - total_strips)
    offs[0] = 0
    for k in range(ns):
        target = lax.rem(me + k, ns)
        pick = 0
        for j in range(BLOCKS_DEV):
            pick = jnp.where(owner[0, me * BLOCKS_DEV + j] == target, j, pick)
        chosen[k] = pick

    hear_hello(everyone)
    place_copies = [
        remote(
            place.at[:, pl.ds(row_dev, row_reach)],
            place.at[:, pl.ds(0, row_reach)],
            sem_s.at[6, 0], sem_r.at[6, 0], "sixteen", ns, 1,
        ),
        remote(
            place.at[:, pl.ds(row_reach, row_reach)],
            place.at[:, pl.ds(row_reach + row_dev, row_reach)],
            sem_s.at[6, 1], sem_r.at[6, 1], "sixteen", ns, ns - 1,
        ),
    ]
    obs_copies = edge_copies(obs, edge, reach, ns, sem_s.at[7], sem_r.at[7])
    row_copies = edge_copies(row_eff, row_edge, reach, ns, sem_s.at[8], sem_r.at[8])
    start(place_copies)
    start(obs_copies)

    seen_t = turned(seen, lanes)
    for r in range(rows):
        weight[r] = beside(across(seen_t, 2 * r, full), across(seen_t, 2 * r + 1, full))
    one_scale = scale_in[...]
    scale[...] = jnp.concatenate([one_scale, one_scale], axis=1)
    inv = 1.0 / scale[...]
    row_eff[...] = jnp.zeros_like(row_eff)
    col_eff[...] = jnp.zeros_like(col_eff)

    spread = 2.0 * strip_rows
    cutoff = 6.0 * strip_rows
    ratio = ROOT_THREE * cutoff / spread
    unit = (4.0 * ratio * SILL_TERM) ** (1.0 / 6.0)

    def prepare_places():
        coords[0] = (place[0] - (me * row_dev + row_dev // 2).astype(F32)) * (unit / cutoff)
        coords[1] = (place[1] - (group_me * cols + cols // 2).astype(F32)) * (unit / cutoff)
        for c in range(2):
            t = turned(coords[c, pl.ds(row_reach, row_dev)], lanes)
            for r in range(row_dev):
                cb[c, r] = across(t, r, full)
        for c in range(2):
            for pair in range(pairs):
                a = [
                    coords[c, pl.ds(2 * pair + parity, oth.shape[2], stride=strip_rows), :]
                    for parity in range(2)
                ]
                for i, s in enumerate(starts):
                    x = pltpu.roll(a[0], (cols - s) % cols, 1)
                    y = pltpu.roll(a[1], (cols + span - s) % cols, 1)
                    oth[i, c, :, pair * lanes : (pair + 1) * lanes] = beside(x, y)

    def build_tile(t, carry):
        block, i = t // groups, lax.rem(t, groups)
        at = pl.multiple_of(i * GROUP, GROUP)
        first = pl.multiple_of(block * strip_rows, strip_rows)
        row_here = cb[0, pl.ds(first, strip_rows), pl.ds(at, GROUP), :].reshape(tile_rows, lanes)
        col_here = cb[1, pl.ds(first, strip_rows), pl.ds(at, GROUP), :].reshape(tile_rows, lanes)
        for n in range(NEIGHBOURS + 1):
            h = block + REACH + offs[n]
            row_line = oth[i, 0, pl.ds(h, 1), :]
            col_line = oth[i, 1, pl.ds(h, 1), :]
            for part in range(wide // lanes):
                cut = slice(part * lanes, (part + 1) * lanes)
                row_gap = row_line[:, cut] - row_here
                col_gap = col_line[:, cut] - col_here
                square = row_gap * row_gap + col_gap * col_gap
                if n == 0:
                    distance = square * lax.rsqrt(jnp.maximum(square, 1e-30))
                else:
                    distance = square * lax.rsqrt(square)
                fading = jnp.maximum(unit - distance, 0.0)
                fading = fading * fading
                fading = fading * fading
                decay = jnp.exp2(distance * (-ratio * LOG2E / unit))
                lead = (distance + unit / ratio) * (distance + unit / 4.0)
                kernel = (lead * decay) * fading
                if n == 0:
                    kernel = kernel * (NEIGHBOURS + 1.0)
                high = kernel.astype(jnp.bfloat16)
                low = (kernel - high.astype(F32)).astype(jnp.bfloat16)
                base = n * wide + part * lanes
                tiles[block, i, 0:tile_rows, base : base + lanes] = high
                tiles[block, i, tile_rows : 2 * tile_rows, base : base + lanes] = low
        return carry

    steps = BLOCKS_DEV * groups
    quarter = steps // (2 * SWEEPS)

    def build_some(part):
        lax.fori_loop(part * quarter, (part + 1) * quarter, build_tile, 0)

    edge_value = HUBER_EDGE
    for sweep in range(SWEEPS):
        row_buf = (row_buf0, row_buf1)[min(sweep, 1)]
        col_buf = (col_buf0, col_buf1)[min(sweep, 1)]

        def clipped(r):
            value = (obs[r] - row_eff[pl.ds(r, 1)] - col_eff[...]) * inv
            return weight[r] * jnp.clip(value, -edge_value, edge_value)

        def row_step(r, carry):
            row_buf[0, pl.ds(r, 1)] = jnp.sum(clipped(r), axis=0, keepdims=True)
            if sweep == 0:
                row_buf[0, pl.ds(rows + r, 1)] = jnp.sum(weight[r], axis=0, keepdims=True)
            return carry

        lax.fori_loop(0, rows, row_step, 0)
        sums = spread_copies(row_buf, "wide", nw, sem_s.at[sweep], sem_r.at[sweep])
        start(sums)
        if sweep == 0:
            wait(place_copies)
            prepare_places()
        build_some(2 * sweep)
        wait(sums)
        total = gathered_sum(row_buf, "wide", nw)
        if sweep == 0:
            row_cnt[...] = jnp.maximum(total[rows:], 1.0)
        row_eff[...] = row_eff[...] + scale[...] * total[:rows] / row_cnt[...]
        if sweep == SWEEPS - 1:
            start(row_copies)

        def col_step(r, carry):
            return carry + clipped(r)

        part = fold(lax.fori_loop(0, rows, col_step, jnp.zeros(full, F32)))
        col_buf[0, pl.ds(0, half)] = beside(part[:half], part[half:])
        if sweep == 0:
            count = jnp.sum(seen, axis=0, keepdims=True)
            col_buf[0, pl.ds(half, 8)] = jnp.broadcast_to(count, (8, cols))
        sums = spread_copies(col_buf, "sixteen", ns, sem_s.at[2 + sweep], sem_r.at[2 + sweep])
        start(sums)
        build_some(2 * sweep + 1)
        wait(sums)
        total = gathered_sum(col_buf, "sixteen", ns)
        if sweep == 0:
            count = jnp.broadcast_to(total[half : half + 1], full).T
            col_cnt[...] = jnp.maximum(count, 1.0)
        y = total[:half]
        z = swap(y)
        both = jnp.concatenate([beside(y, z), beside(z, y)], axis=0)
        col_eff[...] = col_eff[...] + scale[...] * both / col_cnt[...]

    wait(obs_copies)

    def remain(r, carry):
        obs[r] = weight[r] * (obs[r] - row_eff[pl.ds(r, 1)] - col_eff[...])
        return carry

    lax.fori_loop(0, rows, remain, 0)
    p = obs

    def stage(staged, source):
        def one(k, carry):
            for pair in range(pairs):
                staged[k, pair] = source[chosen[k] * pairs + pair]
            return carry

        lax.fori_loop(0, ns, one, 0)

    stage(staged_p, p)
    p_copies = exchange_copies(staged_p, recv_p, ns, exch_s.at[0], exch_r.at[0])
    start(p_copies)

    def windows(source, first, h):
        for pair in range(pairs):
            x = source[first + pair]
            z = swap(x)
            low = low_lanes(x)
            for parity in range(2):
                y = jnp.where(low, x, z) if parity == 0 else jnp.where(low, z, x)
                high = y.astype(jnp.bfloat16).astype(F32)
                both = jnp.where(low, high, y - high)
                win[0, h, 2 * pair + parity] = both.astype(jnp.bfloat16)
                win[1, h, 2 * pair + parity, 0 : cols - GROUP] = both[
                    GROUP // 2 : cols - GROUP // 2
                ].astype(jnp.bfloat16)

    def own_windows(source):
        def one(b, carry):
            windows(source, b * pairs, REACH + b)
            return carry

        lax.fori_loop(0, BLOCKS_DEV, one, 0)

    def edge_windows(source):
        def one(b, carry):
            windows(source, b * pairs, b)
            windows(source, reach + b * pairs, REACH + BLOCKS_DEV + b)
            return carry

        lax.fori_loop(0, REACH, one, 0)

    own_windows(p)
    wait(row_copies)
    seen_t = turned(place[2], lanes)
    for t in range(reach):
        for at, r in ((t, t), (reach + t, reach + rows + t)):
            there = beside(across(seen_t, 2 * r, full), across(seen_t, 2 * r + 1, full))
            edge[at] = there * (edge[at] - row_edge[pl.ds(at, 1)] - col_eff[...])
    edge_windows(edge)
    dots[...] = jnp.zeros_like(dots)

    def apply(block, own_of, store):
        for i, s in enumerate(starts):
            shifted = (s % GROUP) // (GROUP // 2)
            base = s - shifted * (GROUP // 2)
            acc = jnp.zeros((2 * tile_rows, lanes), F32)
            for n in range(NEIGHBOURS + 1):
                h = block + REACH + offs[n]
                acc = acc + jnp.dot(
                    tiles[block, i, :, n * wide : (n + 1) * wide],
                    win[shifted, h, :, base : base + span, :].reshape(wide, lanes),
                    preferred_element_type=F32,
                )
            y = fold(acc[:tile_rows] + acc[tile_rows:])
            for pair in range(pairs):
                even = y[(2 * pair) * GROUP : (2 * pair + 1) * GROUP]
                odd = y[(2 * pair + 1) * GROUP : (2 * pair + 2) * GROUP]
                own = own_of(pair, i * GROUP)
                store(pair, i * GROUP, own, NUGGET_TERM * own + beside(even, odd))

    def gather_dot(k, x, y):
        z = x * y
        dots[k] = dots[k] + (z[: GROUP // 2] + z[GROUP // 2 :])

    def q_copies(t):
        return [
            remote(
                q.at[pl.ds((REACH + t) * pairs, pairs)],
                q_edge.at[pl.ds(t * pairs, pairs)],
                halo_s.at[0, t], halo_r.at[0, t], "sixteen", ns, 1,
            ),
            remote(
                q.at[pl.ds(t * pairs, pairs)],
                q_edge.at[pl.ds(reach + t * pairs, pairs)],
                halo_s.at[1, t], halo_r.at[1, t], "sixteen", ns, ns - 1,
            ),
        ]

    def first_block(block):
        def own_of(pair, at):
            return p[block * pairs + pair, at : at + GROUP, :]

        def store(pair, at, own, value):
            q[block * pairs + pair, at : at + GROUP, :] = value
            gather_dot(0, own, own)
            gather_dot(1, own, value)
            gather_dot(2, value, value)

        apply(block, own_of, store)

    def first_pass(t, carry):
        def one(side, inner):
            first_block(side * REACH + t)
            return inner

        lax.fori_loop(0, 2, one, 0)
        start(q_copies(t))
        return carry

    lax.fori_loop(0, REACH, first_pass, 0)

    stage(staged_q, q)
    q_exchange = exchange_copies(staged_q, recv_q, ns, exch_s.at[1], exch_r.at[1])
    start(q_exchange)
    own_windows(q)
    for t in range(REACH):
        wait(q_copies(t))
    edge_windows(q_edge)

    w_copies = exchange_copies(staged_w, recv_w, ns, exch_s.at[2], exch_r.at[2])
    one_each = ns == BLOCKS_DEV

    def second_block(g, carry):
        slot = lax.rem(g + 1, BLOCKS_DEV)
        block = chosen[slot] if one_each else g

        def own_of(pair, at):
            return q[block * pairs + pair, at : at + GROUP, :]

        def store(pair, at, own, value):
            gather_dot(3, own, value)
            if one_each:
                staged_w[slot, pair, at : at + GROUP, :] = value
            else:
                edge[g * pairs + pair, at : at + GROUP, :] = value

        apply(block, own_of, store)
        if one_each:
            for k in range(ns):

                @pl.when(g == (k - 1) % ns)
                def _(k=k):
                    w_copies[k].start()

        return carry

    lax.fori_loop(0, BLOCKS_DEV, second_block, 0)
    if not one_each:
        stage(staged_w, edge)
        start(w_copies)

    for k in range(4):
        dot_w[0, k : k + 1] = jnp.sum(fold(dots[k]), axis=0, keepdims=True)
    dot_w[0, 4:8] = jnp.zeros((4, lanes), F32)
    sums = spread_copies(dot_w, "wide", nw, sem_s.at[4], sem_r.at[4])
    start(sums)
    wait(sums)
    dot_s[0] = gathered_sum(dot_w, "wide", nw)
    sums = spread_copies(dot_s, "sixteen", ns, sem_s.at[5], sem_r.at[5])
    start(sums)
    wait(sums)
    total = gathered_sum(dot_s, "sixteen", ns)
    m0, m1, m2, m3 = (total[k : k + 1] for k in range(4))
    alpha = m0 / m1
    norm = (m0 - 2.0 * alpha * m1) + alpha * alpha * m2
    grown = 1.0 + norm / m0
    bend = grown * (grown * m1 - 2.0 * alpha * m2) + alpha * alpha * m3
    second = norm / bend
    near = alpha + second * grown
    far = second * alpha

    def slot_of(j):
        return lax.rem(me - j + ns, ns) if static_came else came[j]

    def put(target, j, pair, value):
        value = value.T
        for parity in range(2):
            at = (2 * pair + parity) * cols
            target[:, j, at : at + cols] = value[parity * fields : (parity + 1) * fields]

    wait(p_copies)
    wait(q_exchange)
    for j in range(BLOCKS_DEV):
        k = slot_of(j)
        for pair in range(pairs):
            put(out, j, pair, near * recv_p[k, pair] - far * recv_q[k, pair])
    wait(w_copies)
    for j in range(BLOCKS_DEV):
        k = slot_of(j)
        for pair in range(pairs):
            put(
                rest, j, pair,
                (recv_p[k, pair] - near * recv_q[k, pair]) + far * recv_w[k, pair],
            )


def owned_table(group_map, owners, per_owner):
    total_strips = group_map.shape[0]
    member = (group_map[None, :] == jnp.arange(owners, dtype=jnp.int32)[:, None]).astype(jnp.int32)
    ranked = jnp.cumsum(member, axis=1, dtype=jnp.int32) - 1
    slot_hit = (ranked[:, :, None] == jnp.arange(per_owner, dtype=jnp.int32)[None, None, :]).astype(
        jnp.int32
    ) * member[:, :, None]
    numbers = jnp.arange(total_strips, dtype=jnp.int32)
    return jnp.sum(slot_hit * numbers[None, :, None], axis=1, dtype=jnp.int32)


def on_device(observations, huber_scale, observed, jitter, owner_map, neighbours):
    fields, row_dev, col_dev = observations.shape
    nw, ns = lax.axis_size("wide"), lax.axis_size("sixteen")
    strip_rows = BLOCK // col_dev
    rows, lanes = row_dev // 2, 2 * fields
    pairs = strip_rows // 2
    reach = REACH * pairs
    shape = jax.ShapeDtypeStruct

    cut = 6 * strip_rows
    span = GROUP + 2 * cut
    starts = tuple(
        min(max(GROUP * i - cut, 0), col_dev - span) for i in range(col_dev // GROUP)
    )
    groups = len(starts)
    wide = strip_rows * span
    blocks_halo = BLOCKS_DEV + 2 * REACH

    static_came = ns == BLOCKS_DEV
    if static_came:
        came = jnp.zeros((BLOCKS_DEV,), jnp.int32)
    else:
        my_place = lax.axis_index("sixteen")
        table = owned_table(owner_map[0], ns, BLOCKS_DEV)
        my_ids = lax.dynamic_index_in_dim(table, my_place, 0, keepdims=False)
        came = (my_place - my_ids // BLOCKS_DEV + ns) % ns

    most = max(nw, ns)
    vm = lambda *s: pltpu.VMEM(s, F32)
    moved = (ns, pairs, col_dev, lanes)
    field = (rows, col_dev, lanes)
    place_rows = row_dev + 4 * reach
    out_shape = shape((fields, BLOCKS_DEV, BLOCK), F32)
    solution_now, residual_now = pl.pallas_call(
        functools.partial(solve_kernel, nw, ns, fields, strip_rows, starts, span, static_came),
        out_shape=(out_shape, out_shape),
        in_specs=[SMEM] * 3 + [VMEM] * 4,
        out_specs=(VMEM, VMEM),
        scratch_shapes=[
            pltpu.SMEM((NEIGHBOURS + 1,), jnp.int32),
            pltpu.SMEM((ns,), jnp.int32),
            vm(*field), vm(*field), vm(2 * reach, col_dev, lanes), vm(*field),
            vm(2 * reach, col_dev, lanes),
            vm(*moved), vm(*moved), vm(*moved), vm(*moved), vm(*moved), vm(*moved),
            pltpu.VMEM((BLOCKS_DEV, groups, 2 * strip_rows * GROUP, (NEIGHBOURS + 1) * wide), jnp.bfloat16),
            pltpu.VMEM((2, blocks_halo, strip_rows, col_dev, lanes), jnp.bfloat16),
            vm(2, row_dev, col_dev, lanes),
            vm(groups, 2, blocks_halo, wide),
            vm(3, place_rows, col_dev),
            vm(2, place_rows, col_dev),
            vm(1, lanes),
            vm(rows, lanes), vm(rows, lanes), vm(col_dev, lanes), vm(col_dev, lanes),
            vm(2 * reach, lanes),
            vm(nw, 2 * rows, lanes), vm(nw, rows, lanes),
            vm(ns, col_dev // 2 + 8, lanes), vm(ns, col_dev // 2, lanes),
            vm(4, 8, lanes), vm(nw, 8, lanes), vm(ns, 8, lanes),
            pltpu.SemaphoreType.DMA((9, most)), pltpu.SemaphoreType.DMA((9, most)),
            pltpu.SemaphoreType.DMA((3, ns)), pltpu.SemaphoreType.DMA((3, ns)),
            pltpu.SemaphoreType.DMA((2, REACH)), pltpu.SemaphoreType.DMA((2, REACH)),
        ],
        compiler_params=pltpu.CompilerParams(
            collective_id=0, has_side_effects=True, vmem_limit_bytes=66 * 1000 * 1000
        ),
    )(
        owner_map,
        neighbours[0].T,
        came,
        observations.reshape(fields * row_dev, col_dev),
        huber_scale.reshape(1, fields),
        observed,
        jitter,
    )
    return solution_now[None, None], residual_now[None, None]


def solution(mesh):
    return jax.shard_map(
        on_device,
        mesh=mesh,
        in_specs=(
            P(None, "sixteen", "wide"),
            P(),
            P("sixteen", "wide"),
            P(None, "sixteen", "wide"),
            P("wide", None),
            P("wide", None, None),
        ),
        out_specs=(P("wide", "sixteen", None, None, None), P("wide", "sixteen", None, None, None)),
        check_vma=False,
    )
```

time: 211 us -> 141 us (0.67)
  the two profiles are of different devices: /device:TPU:10 before, /device:TPU:0 now
where the time goes in v1:
time: 141 us
  Pallas kernels  135 us (96%)
  local copies, waits for them, and re-layouts  5.11 us (4%)
    pallas_call x1, Pallas kernels, on_device(): pl.pallas_call(functools.partial(solve_kernel, nw, ns, fields, strip_rows...  135 us
    unnamed x7, local copies, waits for them, and re-layouts  4.6 us

profile of v1, /device:TPU:0, one launch (start us, length us, event | category | flops | bytes accessed | tf_op | source)
XLA Modules:
  0.0 140.5 jit_solution(5813700951827580173)
XLA Ops:
  0.6 0.0 copy-start.1
  0.6 0.7 copy-done.1
  1.3 0.6 copy.10
  1.9 0.5 broadcast_1_came.2.came
  2.4 134.8 %shard_map.77 = (f32[64,8,512]{2,1,0:T(8,128)}, f32[64,8,512]{2,1,0:T(8,128)}) custom-call(s32[1,64]{1,0:T(1,128)} %owner.1, s32[6,64]{1,0:T(8,128)} %bitcast.12, s32[8]{0:T(128)} %broadcast_1_came.2.came, f32[2048,128]{1,0:T(8,128)} %bitcast.9, f32[1,64]{1,0:T(1,128)} %bitcast.13, s32[32,128]{1,0:T(8,128)} %seen_in.1, f32[2,32,128]{2,1,0:T(8,128)} %jitter_in.1), custom_call_target="tpu_custom_call" | custom-call | tf_op jit(solution)/shard_map/pallas_call | solution.py:578
  137.2 0.0 copy-start
  137.2 2.4 %copy.13 = f32[1,1,64,8,512]{4,3,2,1,0:T(8,128)} copy(f32[1,1,64,8,512]{4,3,2,1,0:T(8,128)} %bitcast.11) | data formatting | bytes 2097152
  139.5 0.0 copy-done
  139.5 1.0 copy.14
Async XLA Ops:
  0.6 0.7 copy-start.1
  137.2 2.4 %copy-start = (f32[64,8,512]{2,1,0:T(8,128)S(1)}, f32[64,8,512]{2,1,0:T(8,128)}, u32[]{:S(2)}) copy-start(f32[64,8,512]{2,1,0:T(8,128)} %get-tuple-element.5) | copy-start | bytes 3145732

commit v2 on v1

--- a/solution.py
+++ b/solution.py
@@ -135,13 +135,15 @@
     out, rest,
     offs, chosen,
     obs, weight, edge, q, q_edge, staged_p, recv_p, staged_q, recv_q, staged_w, recv_w,
-    tiles, win, cb, oth, place, coords,
-    scale, row_eff, row_cnt, col_eff, col_cnt, row_edge, row_buf0, row_buf1, col_buf0, col_buf1,
+    staged_m, recv_m, tiles, win, cb, oth, place, coords,
+    scale, row_eff, row_cnt, col_eff, col_cnt, row_edge, row_buf0, row_buf1,
+    col_part, col_send0, col_send1, col_got0, col_got1, col_all0, col_all1,
     dots, dot_w, dot_s,
-    sem_s, sem_r, exch_s, exch_r, halo_s, halo_r,
+    sem_s, sem_r, exch_s, exch_r, obs_s, obs_r, halo_s, halo_r,
 ):
     rows, cols, lanes = obs.shape
     half = cols // 2
+    chunk = half // ns
     pairs = strip_rows // 2
     reach = REACH * pairs
     row_dev = 2 * rows
@@ -175,7 +177,7 @@
     place[2, pl.ds(row_reach, row_dev)] = seen
 
     for n in range(NEIGHBOURS):
-        other = listed[n, 0]
+        other = listed[n, 0, 0]
         offs[n + 1] = jnp.where(other < total_strips // 2, other, other - total_strips)
     offs[0] = 0
     for k in range(ns):
@@ -198,11 +200,45 @@
             sem_s.at[6, 1], sem_r.at[6, 1], "sixteen", ns, ns - 1,
         ),
     ]
-    obs_copies = edge_copies(obs, edge, reach, ns, sem_s.at[7], sem_r.at[7])
+
+    def halo_copies(source, target, size, send, recv, t):
+        return [
+            remote(
+                source.at[pl.ds(rows - reach + t * size, size)],
+                target.at[pl.ds(t * size, size)],
+                send.at[0, t], recv.at[0, t], "sixteen", ns, 1,
+            ),
+            remote(
+                source.at[pl.ds(t * size, size)],
+                target.at[pl.ds(reach + t * size, size)],
+                send.at[1, t], recv.at[1, t], "sixteen", ns, ns - 1,
+            ),
+        ]
+
+    obs_copies = [halo_copies(obs, edge, 1, obs_s, obs_r, t) for t in range(reach)]
     row_copies = edge_copies(row_eff, row_edge, reach, ns, sem_s.at[8], sem_r.at[8])
     start(place_copies)
-    start(obs_copies)
-
+
+    def stage(staged, source):
+        def one(k, carry):
+            for pair in range(pairs):
+                staged[k, pair] = source[chosen[k] * pairs + pair]
+            return carry
+
+        lax.fori_loop(0, ns, one, 0)
+
+    stage(staged_p, obs)
+    p_copies = exchange_copies(staged_p, recv_p, ns, exch_s.at[0], exch_r.at[0])
+
+    near_first = p_copies[2::2]
+    bulk = [
+        p_copies[:1] + sum(obs_copies[0:3], []) + near_first[0::3],
+        sum(obs_copies[3:4], []),
+        sum(obs_copies[4:6], []) + near_first[1::3],
+        sum(obs_copies[6:7], []),
+        sum(obs_copies[7:8], []) + near_first[2::3] + p_copies[1::2],
+    ]
+    start(bulk[0])
     seen_t = turned(seen, lanes)
     for r in range(rows):
         weight[r] = beside(across(seen_t, 2 * r, full), across(seen_t, 2 * r + 1, full))
@@ -270,15 +306,18 @@
         return carry
 
     steps = BLOCKS_DEV * groups
-    quarter = steps // (2 * SWEEPS)
+    shares = (0, 8, 20, 32, 40, 52, 64)
 
     def build_some(part):
-        lax.fori_loop(part * quarter, (part + 1) * quarter, build_tile, 0)
-
+        lax.fori_loop(shares[part] * steps // 64, shares[part + 1] * steps // 64, build_tile, 0)
+
+    m_copies = exchange_copies(staged_m, recv_m, ns, exch_s.at[3], exch_r.at[3])
     edge_value = HUBER_EDGE
     for sweep in range(SWEEPS):
         row_buf = (row_buf0, row_buf1)[min(sweep, 1)]
-        col_buf = (col_buf0, col_buf1)[min(sweep, 1)]
+        col_send = (col_send0, col_send1)[min(sweep, 1)]
+        col_got = (col_got0, col_got1)[min(sweep, 1)]
+        col_all = (col_all0, col_all1)[min(sweep, 1)]
 
         def clipped(r):
             value = (obs[r] - row_eff[pl.ds(r, 1)] - col_eff[...]) * inv
@@ -296,7 +335,7 @@
         if sweep == 0:
             wait(place_copies)
             prepare_places()
-        build_some(2 * sweep)
+        build_some(3 * sweep)
         wait(sums)
         total = gathered_sum(row_buf, "wide", nw)
         if sweep == 0:
@@ -305,28 +344,60 @@
         if sweep == SWEEPS - 1:
             start(row_copies)
 
+            def describe(k, carry):
+                for pair in range(pairs):
+                    staged_m[k, pair : pair + 1] = row_eff[pl.ds(chosen[k] * pairs + pair, 1)]
+                for r in range(strip_rows):
+                    at = pairs + r
+                    staged_m[k, at : at + 1] = place[2, pl.ds(row_reach + chosen[k] * strip_rows + r, 1)]
+                return carry
+
+            staged_m[...] = jnp.zeros_like(staged_m)
+            lax.fori_loop(0, ns, describe, 0)
+            start(m_copies)
+
         def col_step(r, carry):
             return carry + clipped(r)
 
         part = fold(lax.fori_loop(0, rows, col_step, jnp.zeros(full, F32)))
-        col_buf[0, pl.ds(0, half)] = beside(part[:half], part[half:])
+        col_part[0:half] = beside(part[:half], part[half:])
+        count = jnp.sum(seen, axis=0, keepdims=True)
+        for k in range(ns):
+            owner_of = lax.rem(me + k, ns)
+            col_send[k, 0:chunk] = col_part[pl.ds(pl.multiple_of(owner_of * chunk, chunk), chunk)]
+            col_send[k, chunk : chunk + 8] = jnp.broadcast_to(count, (8, cols))
+        col_got[0] = col_send[0]
+        sums = [
+            remote(
+                col_send.at[k], col_got.at[k],
+                sem_s.at[2 + sweep, k], sem_r.at[2 + sweep, k], "sixteen", ns, k,
+            )
+            for k in range(1, ns)
+        ]
+        start(sums)
+        start(bulk[2 * sweep + 1])
+        build_some(3 * sweep + 1)
+        wait(sums)
+        total = gathered_sum(col_got, "sixteen", ns)
+        col_all[0] = total[:chunk]
         if sweep == 0:
-            count = jnp.sum(seen, axis=0, keepdims=True)
-            col_buf[0, pl.ds(half, 8)] = jnp.broadcast_to(count, (8, cols))
-        sums = spread_copies(col_buf, "sixteen", ns, sem_s.at[2 + sweep], sem_r.at[2 + sweep])
+            counts = jnp.broadcast_to(total[chunk : chunk + 1], full).T
+            col_cnt[...] = jnp.maximum(counts, 1.0)
+        sums = spread_copies(col_all, "sixteen", ns, sem_s.at[9 + sweep], sem_r.at[9 + sweep])
         start(sums)
-        build_some(2 * sweep + 1)
+        start(bulk[2 * sweep + 2])
+        build_some(3 * sweep + 2)
         wait(sums)
-        total = gathered_sum(col_buf, "sixteen", ns)
-        if sweep == 0:
-            count = jnp.broadcast_to(total[half : half + 1], full).T
-            col_cnt[...] = jnp.maximum(count, 1.0)
+        total = jnp.concatenate(
+            [col_all[lax.rem(me - o + ns, ns)] for o in range(ns)], axis=0
+        )
         y = total[:half]
         z = swap(y)
         both = jnp.concatenate([beside(y, z), beside(z, y)], axis=0)
         col_eff[...] = col_eff[...] + scale[...] * both / col_cnt[...]
 
-    wait(obs_copies)
+    for copies in obs_copies:
+        wait(copies)
 
     def remain(r, carry):
         obs[r] = weight[r] * (obs[r] - row_eff[pl.ds(r, 1)] - col_eff[...])
@@ -334,18 +405,6 @@
 
     lax.fori_loop(0, rows, remain, 0)
     p = obs
-
-    def stage(staged, source):
-        def one(k, carry):
-            for pair in range(pairs):
-                staged[k, pair] = source[chosen[k] * pairs + pair]
-            return carry
-
-        lax.fori_loop(0, ns, one, 0)
-
-    stage(staged_p, p)
-    p_copies = exchange_copies(staged_p, recv_p, ns, exch_s.at[0], exch_r.at[0])
-    start(p_copies)
 
     def windows(source, first, h):
         for pair in range(pairs):
@@ -410,18 +469,7 @@
         dots[k] = dots[k] + (z[: GROUP // 2] + z[GROUP // 2 :])
 
     def q_copies(t):
-        return [
-            remote(
-                q.at[pl.ds((REACH + t) * pairs, pairs)],
-                q_edge.at[pl.ds(t * pairs, pairs)],
-                halo_s.at[0, t], halo_r.at[0, t], "sixteen", ns, 1,
-            ),
-            remote(
-                q.at[pl.ds(t * pairs, pairs)],
-                q_edge.at[pl.ds(reach + t * pairs, pairs)],
-                halo_s.at[1, t], halo_r.at[1, t], "sixteen", ns, ns - 1,
-            ),
-        ]
+        return halo_copies(q, q_edge, pairs, halo_s, halo_r, t)
 
     def first_block(block):
         def own_of(pair, at):
@@ -448,14 +496,24 @@
 
     stage(staged_q, q)
     q_exchange = exchange_copies(staged_q, recv_q, ns, exch_s.at[1], exch_r.at[1])
-    start(q_exchange)
+    start(q_exchange[0::2])
     own_windows(q)
+    wait(p_copies)
+    wait(m_copies)
+    facts = turned(recv_m[...].reshape(ns * 8, cols), lanes)
+    for k in range(ns):
+        for pair in range(pairs):
+            at = 8 * k + pairs + 2 * pair
+            there = beside(across(facts, at, full), across(facts, at + 1, full))
+            recv_p[k, pair] = there * (recv_p[k, pair] - recv_m[k, pair : pair + 1] - col_eff[...])
     for t in range(REACH):
         wait(q_copies(t))
+    start(q_exchange[1::2])
     edge_windows(q_edge)
 
     w_copies = exchange_copies(staged_w, recv_w, ns, exch_s.at[2], exch_r.at[2])
     one_each = ns == BLOCKS_DEV
+    held = 1 + ns // 2 if one_each else 0
 
     def second_block(g, carry):
         slot = lax.rem(g + 1, BLOCKS_DEV)
@@ -473,9 +531,9 @@
 
         apply(block, own_of, store)
         if one_each:
-            for k in range(ns):
-
-                @pl.when(g == (k - 1) % ns)
+            for k in range(1, held):
+
+                @pl.when(g == k - 1)
                 def _(k=k):
                     w_copies[k].start()
 
@@ -484,7 +542,6 @@
     lax.fori_loop(0, BLOCKS_DEV, second_block, 0)
     if not one_each:
         stage(staged_w, edge)
-        start(w_copies)
 
     for k in range(4):
         dot_w[0, k : k + 1] = jnp.sum(fold(dots[k]), axis=0, keepdims=True)
@@ -495,6 +552,7 @@
     dot_s[0] = gathered_sum(dot_w, "wide", nw)
     sums = spread_copies(dot_s, "sixteen", ns, sem_s.at[5], sem_r.at[5])
     start(sums)
+    start((w_copies[:1] if one_each else []) + w_copies[held:])
     wait(sums)
     total = gathered_sum(dot_s, "sixteen", ns)
     m0, m1, m2, m3 = (total[k : k + 1] for k in range(4))
@@ -509,26 +567,26 @@
     def slot_of(j):
         return lax.rem(me - j + ns, ns) if static_came else came[j]
 
-    def put(target, j, pair, value):
-        value = value.T
-        for parity in range(2):
-            at = (2 * pair + parity) * cols
-            target[:, j, at : at + cols] = value[parity * fields : (parity + 1) * fields]
-
-    wait(p_copies)
+    def put(target, source):
+        for j in range(BLOCKS_DEV):
+            k = slot_of(j)
+            for pair in range(pairs):
+                value = source[k, pair]
+                for parity in range(2):
+                    at = (2 * pair + parity) * cols
+                    target[:, j, at : at + cols] = value[parity * fields : (parity + 1) * fields]
+
     wait(q_exchange)
-    for j in range(BLOCKS_DEV):
-        k = slot_of(j)
+    for k in range(ns):
         for pair in range(pairs):
-            put(out, j, pair, near * recv_p[k, pair] - far * recv_q[k, pair])
-    wait(w_copies)
-    for j in range(BLOCKS_DEV):
-        k = slot_of(j)
+            staged_q[k, pair] = (near * recv_p[k, pair] - far * recv_q[k, pair]).T
+            recv_p[k, pair] = recv_p[k, pair] - near * recv_q[k, pair]
+    put(out, staged_q)
+    for k in range(ns):
+        wait(w_copies[k : k + 1])
         for pair in range(pairs):
-            put(
-                rest, j, pair,
-                (recv_p[k, pair] - near * recv_q[k, pair]) + far * recv_w[k, pair],
-            )
+            recv_w[k, pair] = (recv_p[k, pair] + far * recv_w[k, pair]).T
+    put(rest, recv_w)
 
 
 def owned_table(group_map, owners, per_owner):
@@ -562,7 +620,7 @@
 
     static_came = ns == BLOCKS_DEV
     if static_came:
-        came = jnp.zeros((BLOCKS_DEV,), jnp.int32)
+        came = owner_map
     else:
         my_place = lax.axis_index("sixteen")
         table = owned_table(owner_map[0], ns, BLOCKS_DEV)
@@ -572,6 +630,7 @@
     most = max(nw, ns)
     vm = lambda *s: pltpu.VMEM(s, F32)
     moved = (ns, pairs, col_dev, lanes)
+    piece = (ns, col_dev // 2 // ns + 8, lanes)
     field = (rows, col_dev, lanes)
     place_rows = row_dev + 4 * reach
     out_shape = shape((fields, BLOCKS_DEV, BLOCK), F32)
@@ -586,6 +645,7 @@
             vm(*field), vm(*field), vm(2 * reach, col_dev, lanes), vm(*field),
             vm(2 * reach, col_dev, lanes),
             vm(*moved), vm(*moved), vm(*moved), vm(*moved), vm(*moved), vm(*moved),
+            vm(ns, 8, lanes), vm(ns, 8, lanes),
             pltpu.VMEM((BLOCKS_DEV, groups, 2 * strip_rows * GROUP, (NEIGHBOURS + 1) * wide), jnp.bfloat16),
             pltpu.VMEM((2, blocks_halo, strip_rows, col_dev, lanes), jnp.bfloat16),
             vm(2, row_dev, col_dev, lanes),
@@ -596,18 +656,21 @@
             vm(rows, lanes), vm(rows, lanes), vm(col_dev, lanes), vm(col_dev, lanes),
             vm(2 * reach, lanes),
             vm(nw, 2 * rows, lanes), vm(nw, rows, lanes),
-            vm(ns, col_dev // 2 + 8, lanes), vm(ns, col_dev // 2, lanes),
+            vm(col_dev // 2, lanes),
+            vm(*piece), vm(*piece), vm(*piece), vm(*piece),
+            vm(ns, col_dev // 2 // ns, lanes), vm(ns, col_dev // 2 // ns, lanes),
             vm(4, 8, lanes), vm(nw, 8, lanes), vm(ns, 8, lanes),
-            pltpu.SemaphoreType.DMA((9, most)), pltpu.SemaphoreType.DMA((9, most)),
-            pltpu.SemaphoreType.DMA((3, ns)), pltpu.SemaphoreType.DMA((3, ns)),
+            pltpu.SemaphoreType.DMA((11, most)), pltpu.SemaphoreType.DMA((11, most)),
+            pltpu.SemaphoreType.DMA((4, ns)), pltpu.SemaphoreType.DMA((4, ns)),
+            pltpu.SemaphoreType.DMA((2, reach)), pltpu.SemaphoreType.DMA((2, reach)),
             pltpu.SemaphoreType.DMA((2, REACH)), pltpu.SemaphoreType.DMA((2, REACH)),
         ],
         compiler_params=pltpu.CompilerParams(
-            collective_id=0, has_side_effects=True, vmem_limit_bytes=66 * 1000 * 1000
+            collective_id=0, has_side_effects=True, vmem_limit_bytes=57 * 1000 * 1000 if static_came else 66 * 1000 * 1000
         ),
     )(
         owner_map,
-        neighbours[0].T,
+        jnp.transpose(neighbours, (2, 0, 1)),
         came,
         observations.reshape(fields * row_dev, col_dev),
         huber_scale.reshape(1, fields),

time: 141 us -> 124 us (0.88)
  the two profiles are of different devices: /device:TPU:0 before, /device:TPU:10 now
where the time goes in v2:
time: 124 us; the launch traced here: 122 us
  Pallas kernels  118 us (95%)
  local copies, waits for them, and re-layouts  3.32 us (3%)
    pallas_call x1, Pallas kernels, on_device(): pl.pallas_call(functools.partial(solve_kernel, nw, ns, fields, strip_rows...  118 us
    unnamed x4, local copies, waits for them, and re-layouts  3.32 us

profile of v2, /device:TPU:10, one launch (start us, length us, event | category | flops | bytes accessed | tf_op | source)
XLA Modules:
  0.0 121.8 jit_solution(13479307551396148591)
XLA Ops:
  0.6 117.8 %shard_map.77 = (f32[64,8,512]{2,1,0:T(8,128)}, f32[64,8,512]{2,1,0:T(8,128)}) custom-call(s32[1,64]{1,0:T(1,128)} %came.1, s32[6,1,64]{2,1,0:T(1,128)} %bitcast.8, s32[1,64]{1,0:T(1,128)} %came.1, f32[2048,128]{1,0:T(8,128)} %bitcast.5, f32[1,64]{1,0:T(1,128)} %bitcast.9, s32[32,128]{1,0:T(8,128)} %seen_in.1, f32[2,32,128]{2,1,0:T(8,128)} %jitter_in.1), custom_call_target="tpu_custom_call" | custom-call | tf_op jit(solution)/shard_map/pallas_call | solution.py:637
  118.4 0.0 copy-start
  118.4 2.4 %copy.10 = f32[1,1,64,8,512]{4,3,2,1,0:T(8,128)} copy(f32[1,1,64,8,512]{4,3,2,1,0:T(8,128)} %bitcast.7) | data formatting | bytes 2097152
  120.8 0.0 copy-done
  120.8 1.0 copy.11
Async XLA Ops:
  118.4 2.4 %copy-start = (f32[64,8,512]{2,1,0:T(8,128)S(1)}, f32[64,8,512]{2,1,0:T(8,128)}, u32[]{:S(2)}) copy-start(f32[64,8,512]{2,1,0:T(8,128)} %get-tuple-element.5) | copy-start | bytes 3145732

commit v3 on v2

--- a/solution.py
+++ b/solution.py
@@ -131,15 +131,15 @@
 
 def solve_kernel(
     nw, ns, fields, strip_rows, starts, span, static_came,
-    owner, listed, came, obs_in, scale_in, seen_in, jitter_in,
+    came, owner_hbm, listed_hbm, obs_hbm, scale_hbm, seen_hbm, jitter_hbm,
     out, rest,
-    offs, chosen,
+    offs, chosen, owner, listed, obs_in, scale_in, seen_in, jitter_in,
     obs, weight, edge, q, q_edge, staged_p, recv_p, staged_q, recv_q, staged_w, recv_w,
-    staged_m, recv_m, tiles, win, cb, oth, place, coords,
+    staged_m, recv_m, tiles, win, cb, oth, own_oth, place, coords,
     scale, row_eff, row_cnt, col_eff, col_cnt, row_edge, row_buf0, row_buf1,
     col_part, col_send0, col_send1, col_got0, col_got1, col_all0, col_all1,
     dots, dot_w, dot_s,
-    sem_s, sem_r, exch_s, exch_r, obs_s, obs_r, halo_s, halo_r,
+    sem_in, sem_s, sem_r, exch_s, exch_r, obs_s, obs_r, halo_s, halo_r,
 ):
     rows, cols, lanes = obs.shape
     half = cols // 2
@@ -150,6 +150,7 @@
     row_reach = 2 * reach
     groups = len(starts)
     wide = strip_rows * span
+    parts = wide // lanes
     tile_rows = strip_rows * GROUP
     total_strips = BLOCKS_DEV * ns
     me = lax.axis_index("sixteen")
@@ -158,6 +159,17 @@
     full = (cols, lanes)
 
     say_hello(everyone)
+    arrivals = [
+        pltpu.make_async_copy(source, target, sem_in.at[k])
+        for k, (source, target) in enumerate(
+            (
+                (obs_hbm, obs_in), (scale_hbm, scale_in), (seen_hbm, seen_in),
+                (jitter_hbm, jitter_in), (owner_hbm, owner), (listed_hbm, listed),
+            )
+        )
+    ]
+    start(arrivals)
+    wait(arrivals)
 
     def pack(r, carry):
         both = jnp.concatenate(
@@ -253,60 +265,77 @@
     ratio = ROOT_THREE * cutoff / spread
     unit = (4.0 * ratio * SILL_TERM) ** (1.0 / 6.0)
 
-    def prepare_places():
-        coords[0] = (place[0] - (me * row_dev + row_dev // 2).astype(F32)) * (unit / cutoff)
-        coords[1] = (place[1] - (group_me * cols + cols // 2).astype(F32)) * (unit / cutoff)
-        for c in range(2):
-            t = turned(coords[c, pl.ds(row_reach, row_dev)], lanes)
-            for r in range(row_dev):
-                cb[c, r] = across(t, r, full)
+    def centred(first, count):
+        at = pl.ds(first, count)
+        coords[0, at] = (place[0, at] - (me * row_dev + row_dev // 2).astype(F32)) * (unit / cutoff)
+        coords[1, at] = (place[1, at] - (group_me * cols + cols // 2).astype(F32)) * (unit / cutoff)
+
+    def lines(target, first, blocks):
         for c in range(2):
             for pair in range(pairs):
                 a = [
-                    coords[c, pl.ds(2 * pair + parity, oth.shape[2], stride=strip_rows), :]
+                    coords[c, pl.ds(first + 2 * pair + parity, blocks, stride=strip_rows), :]
                     for parity in range(2)
                 ]
                 for i, s in enumerate(starts):
                     x = pltpu.roll(a[0], (cols - s) % cols, 1)
                     y = pltpu.roll(a[1], (cols + span - s) % cols, 1)
-                    oth[i, c, :, pair * lanes : (pair + 1) * lanes] = beside(x, y)
-
-    def build_tile(t, carry):
-        block, i = t // groups, lax.rem(t, groups)
-        at = pl.multiple_of(i * GROUP, GROUP)
-        first = pl.multiple_of(block * strip_rows, strip_rows)
-        row_here = cb[0, pl.ds(first, strip_rows), pl.ds(at, GROUP), :].reshape(tile_rows, lanes)
-        col_here = cb[1, pl.ds(first, strip_rows), pl.ds(at, GROUP), :].reshape(tile_rows, lanes)
-        for n in range(NEIGHBOURS + 1):
-            h = block + REACH + offs[n]
-            row_line = oth[i, 0, pl.ds(h, 1), :]
-            col_line = oth[i, 1, pl.ds(h, 1), :]
-            for part in range(wide // lanes):
-                cut = slice(part * lanes, (part + 1) * lanes)
-                row_gap = row_line[:, cut] - row_here
-                col_gap = col_line[:, cut] - col_here
-                square = row_gap * row_gap + col_gap * col_gap
-                if n == 0:
-                    distance = square * lax.rsqrt(jnp.maximum(square, 1e-30))
-                else:
-                    distance = square * lax.rsqrt(square)
-                fading = jnp.maximum(unit - distance, 0.0)
-                fading = fading * fading
-                fading = fading * fading
-                decay = jnp.exp2(distance * (-ratio * LOG2E / unit))
-                lead = (distance + unit / ratio) * (distance + unit / 4.0)
-                kernel = (lead * decay) * fading
-                if n == 0:
-                    kernel = kernel * (NEIGHBOURS + 1.0)
-                high = kernel.astype(jnp.bfloat16)
-                low = (kernel - high.astype(F32)).astype(jnp.bfloat16)
-                base = n * wide + part * lanes
-                tiles[block, i, 0:tile_rows, base : base + lanes] = high
-                tiles[block, i, tile_rows : 2 * tile_rows, base : base + lanes] = low
-        return carry
+                    target[i, c, :, pair * lanes : (pair + 1) * lanes] = beside(x, y)
+
+    def prepare_own():
+        centred(row_reach, row_dev)
+        for c in range(2):
+            t = turned(coords[c, pl.ds(row_reach, row_dev)], lanes)
+            for r in range(row_dev):
+                cb[c, r] = across(t, r, full)
+        lines(own_oth, row_reach, BLOCKS_DEV)
+
+    def prepare_all():
+        centred(0, row_reach)
+        centred(row_reach + row_dev, row_reach)
+        lines(oth, 0, oth.shape[2])
+
+    def tile_builder(source, first_block, members):
+        def build(t, carry):
+            block, i = t // groups, lax.rem(t, groups)
+            at = pl.multiple_of(i * GROUP, GROUP)
+            first = pl.multiple_of(block * strip_rows, strip_rows)
+            row_here = cb[0, pl.ds(first, strip_rows), pl.ds(at, GROUP), :].reshape(tile_rows, lanes)
+            col_here = cb[1, pl.ds(first, strip_rows), pl.ds(at, GROUP), :].reshape(tile_rows, lanes)
+            for n in members:
+                h = block + first_block + (offs[n] if n else 0)
+                row_line = source[i, 0, pl.ds(h, 1), :]
+                col_line = source[i, 1, pl.ds(h, 1), :]
+                for part in range(parts):
+                    cut = slice(part * lanes, (part + 1) * lanes)
+                    row_gap = row_line[:, cut] - row_here
+                    col_gap = col_line[:, cut] - col_here
+                    square = row_gap * row_gap + col_gap * col_gap
+                    if n == 0:
+                        distance = square * lax.rsqrt(jnp.maximum(square, 1e-30))
+                    else:
+                        distance = square * lax.rsqrt(square)
+                    fading = jnp.maximum(unit - distance, 0.0)
+                    fading = fading * fading
+                    fading = fading * fading
+                    decay = jnp.exp2(distance * (-ratio * LOG2E / unit))
+                    lead = (distance + unit / ratio) * (distance + unit / 4.0)
+                    kernel = (lead * decay) * fading
+                    if n == 0:
+                        kernel = kernel * (NEIGHBOURS + 1.0)
+                    high = kernel.astype(jnp.bfloat16)
+                    low = (kernel - high.astype(F32)).astype(jnp.bfloat16)
+                    tiles[block, i, parts * n + part, 0:tile_rows] = high
+                    tiles[block, i, parts * n + part, tile_rows : 2 * tile_rows] = low
+            return carry
+
+        return build
+
+    build_own = tile_builder(own_oth, 0, (0,))
+    build_tile = tile_builder(oth, REACH, tuple(range(1, NEIGHBOURS + 1)))
 
     steps = BLOCKS_DEV * groups
-    shares = (0, 8, 20, 32, 40, 52, 64)
+    shares = (0, 9, 20, 32, 41, 52, 64)
 
     def build_some(part):
         lax.fori_loop(shares[part] * steps // 64, shares[part + 1] * steps // 64, build_tile, 0)
@@ -333,8 +362,10 @@
         sums = spread_copies(row_buf, "wide", nw, sem_s.at[sweep], sem_r.at[sweep])
         start(sums)
         if sweep == 0:
+            prepare_own()
+            lax.fori_loop(0, steps, build_own, 0)
             wait(place_copies)
-            prepare_places()
+            prepare_all()
         build_some(3 * sweep)
         wait(sums)
         total = gathered_sum(row_buf, "wide", nw)
@@ -453,7 +484,9 @@
             for n in range(NEIGHBOURS + 1):
                 h = block + REACH + offs[n]
                 acc = acc + jnp.dot(
-                    tiles[block, i, :, n * wide : (n + 1) * wide],
+                    jnp.concatenate(
+                        [tiles[block, i, parts * n + part] for part in range(parts)], axis=1
+                    ),
                     win[shifted, h, :, base : base + span, :].reshape(wide, lanes),
                     preferred_element_type=F32,
                 )
@@ -483,16 +516,22 @@
 
         apply(block, own_of, store)
 
-    def first_pass(t, carry):
-        def one(side, inner):
-            first_block(side * REACH + t)
-            return inner
-
-        lax.fori_loop(0, 2, one, 0)
-        start(q_copies(t))
+    def first_pass(u, carry):
+        t, side = u // 2, lax.rem(u, 2)
+        first_block(side * REACH + t)
+        up, down = q_copies(t)
+
+        @pl.when(side == 0)
+        def _():
+            down.start()
+
+        @pl.when(side == 1)
+        def _():
+            up.start()
+
         return carry
 
-    lax.fori_loop(0, REACH, first_pass, 0)
+    lax.fori_loop(0, BLOCKS_DEV, first_pass, 0)
 
     stage(staged_q, q)
     q_exchange = exchange_copies(staged_q, recv_q, ns, exch_s.at[1], exch_r.at[1])
@@ -513,7 +552,7 @@
 
     w_copies = exchange_copies(staged_w, recv_w, ns, exch_s.at[2], exch_r.at[2])
     one_each = ns == BLOCKS_DEV
-    held = 1 + ns // 2 if one_each else 0
+    held = 3 if one_each else 0
 
     def second_block(g, carry):
         slot = lax.rem(g + 1, BLOCKS_DEV)
@@ -628,6 +667,7 @@
         came = (my_place - my_ids // BLOCKS_DEV + ns) % ns
 
     most = max(nw, ns)
+    anywhere = pl.BlockSpec(memory_space=pl.ANY)
     vm = lambda *s: pltpu.VMEM(s, F32)
     moved = (ns, pairs, col_dev, lanes)
     piece = (ns, col_dev // 2 // ns + 8, lanes)
@@ -636,20 +676,30 @@
     out_shape = shape((fields, BLOCKS_DEV, BLOCK), F32)
     solution_now, residual_now = pl.pallas_call(
         functools.partial(solve_kernel, nw, ns, fields, strip_rows, starts, span, static_came),
-        out_shape=(out_shape, out_shape),
-        in_specs=[SMEM] * 3 + [VMEM] * 4,
+        out_shape=((vm(*out_shape.shape) if static_came else out_shape),) * 2,
+        in_specs=[anywhere if static_came else SMEM] + [anywhere] * 6,
         out_specs=(VMEM, VMEM),
         scratch_shapes=[
             pltpu.SMEM((NEIGHBOURS + 1,), jnp.int32),
             pltpu.SMEM((ns,), jnp.int32),
+            pltpu.SMEM(owner_map.shape, jnp.int32),
+            pltpu.SMEM((NEIGHBOURS, 1, neighbours.shape[1]), jnp.int32),
+            vm(fields * row_dev, col_dev),
+            vm(1, fields),
+            pltpu.VMEM((row_dev, col_dev), jnp.int32),
+            vm(2, row_dev, col_dev),
             vm(*field), vm(*field), vm(2 * reach, col_dev, lanes), vm(*field),
             vm(2 * reach, col_dev, lanes),
             vm(*moved), vm(*moved), vm(*moved), vm(*moved), vm(*moved), vm(*moved),
             vm(ns, 8, lanes), vm(ns, 8, lanes),
-            pltpu.VMEM((BLOCKS_DEV, groups, 2 * strip_rows * GROUP, (NEIGHBOURS + 1) * wide), jnp.bfloat16),
+            pltpu.VMEM(
+                (BLOCKS_DEV, groups, (NEIGHBOURS + 1) * wide // lanes, 2 * strip_rows * GROUP, lanes),
+                jnp.bfloat16,
+            ),
             pltpu.VMEM((2, blocks_halo, strip_rows, col_dev, lanes), jnp.bfloat16),
             vm(2, row_dev, col_dev, lanes),
             vm(groups, 2, blocks_halo, wide),
+            vm(groups, 2, BLOCKS_DEV, wide),
             vm(3, place_rows, col_dev),
             vm(2, place_rows, col_dev),
             vm(1, lanes),
@@ -660,6 +710,7 @@
             vm(*piece), vm(*piece), vm(*piece), vm(*piece),
             vm(ns, col_dev // 2 // ns, lanes), vm(ns, col_dev // 2 // ns, lanes),
             vm(4, 8, lanes), vm(nw, 8, lanes), vm(ns, 8, lanes),
+            pltpu.SemaphoreType.DMA((6,)),
             pltpu.SemaphoreType.DMA((11, most)), pltpu.SemaphoreType.DMA((11, most)),
             pltpu.SemaphoreType.DMA((4, ns)), pltpu.SemaphoreType.DMA((4, ns)),
             pltpu.SemaphoreType.DMA((2, reach)), pltpu.SemaphoreType.DMA((2, reach)),
@@ -669,9 +720,9 @@
             collective_id=0, has_side_effects=True, vmem_limit_bytes=57 * 1000 * 1000 if static_came else 66 * 1000 * 1000
         ),
     )(
+        came,
         owner_map,
         jnp.transpose(neighbours, (2, 0, 1)),
-        came,
         observations.reshape(fields * row_dev, col_dev),
         huber_scale.reshape(1, fields),
         observed,

time: 124 us -> 118 us (0.952); the launches traced: 122 us -> 117 us
  Pallas kernels: 118 us -> 115 us
  local copies, waits for them, and re-layouts: 3.32 us -> 1.94 us
    pallas_call x1, Pallas kernels: 118 us -> 115 us  [on_device(): pl.pallas_call(functools.partial(solve_kernel, nw, ns, fields, strip_rows...]
    unnamed x4 -> x2, local copies, waits for them, and re-layouts: 3.32 us -> 1.94 us
where the time goes in v3:
time: 118 us; the launch traced here: 117 us
  Pallas kernels  115 us (97%)
  local copies, waits for them, and re-layouts  1.94 us (2%)
    pallas_call x1, Pallas kernels, on_device(): pl.pallas_call(functools.partial(solve_kernel, nw, ns, fields, strip_rows...  115 us

profile of v3, /device:TPU:10, one launch (start us, length us, event | category | flops | bytes accessed | tf_op | source)
XLA Modules:
  0.0 117.4 jit_solution(7971488026070072723)
XLA Ops:
  0.6 114.8 %shard_map.77 = (f32[64,8,512]{2,1,0:T(8,128)S(1)}, f32[64,8,512]{2,1,0:T(8,128)S(1)}) custom-call(s32[1,64]{1,0:T(1,128)} %owner_hbm.1, s32[1,64]{1,0:T(1,128)} %owner_hbm.1, s32[6,1,64]{2,1,0:T(1,128)} %bitcast.8, f32[2048,128]{1,0:T(8,128)} %bitcast.7, f32[1,64]{1,0:T(1,128)} %bitcast.9, s32[32,128]{1,0:T(8,128)} %seen_hbm.1, f32[2,32,128]{2,1,0:T(8,128)} %jitter_hbm.1), custom_call_target="tpu_custom_call" | custom-call | tf_op jit(solution)/shard_map/pallas_call | solution.py:677
  115.4 1.0 copy.10
  116.4 1.0 copy.11

commit v4 on v3

--- a/solution.py
+++ b/solution.py
@@ -179,7 +179,9 @@
         obs[r] = both.T
         return carry
 
-    lax.fori_loop(0, rows, pack, 0)
+    early = 3
+    lax.fori_loop(0, early, pack, 0)
+    lax.fori_loop(rows - reach, rows - reach + early, pack, 0)
 
     row_number = lax.broadcasted_iota(jnp.int32, (row_dev, cols), 0) + me * row_dev
     col_number = lax.broadcasted_iota(jnp.int32, (row_dev, cols), 1) + group_me * cols
@@ -239,16 +241,20 @@
 
         lax.fori_loop(0, ns, one, 0)
 
+    start(sum(obs_copies[:early], []))
+    lax.fori_loop(early, rows - reach, pack, 0)
+    lax.fori_loop(rows - reach + early, rows, pack, 0)
     stage(staged_p, obs)
     p_copies = exchange_copies(staged_p, recv_p, ns, exch_s.at[0], exch_r.at[0])
 
     near_first = p_copies[2::2]
     bulk = [
-        p_copies[:1] + sum(obs_copies[0:3], []) + near_first[0::3],
+        p_copies[:1] + near_first[0::3],
         sum(obs_copies[3:4], []),
-        sum(obs_copies[4:6], []) + near_first[1::3],
+        sum(obs_copies[4:5], []),
         sum(obs_copies[6:7], []),
-        sum(obs_copies[7:8], []) + near_first[2::3] + p_copies[1::2],
+        sum(obs_copies[7:8], [])+near_first[2::3]+p_copies[1::2],
+        sum(obs_copies[5:6], [])+near_first[1::3],
     ]
     start(bulk[0])
     seen_t = turned(seen, lanes)
@@ -335,7 +341,7 @@
     build_tile = tile_builder(oth, REACH, tuple(range(1, NEIGHBOURS + 1)))
 
     steps = BLOCKS_DEV * groups
-    shares = (0, 9, 20, 32, 41, 52, 64)
+    shares = (0, 9, 19, 29, 42, 53, 64)
 
     def build_some(part):
         lax.fori_loop(shares[part] * steps // 64, shares[part + 1] * steps // 64, build_tile, 0)
@@ -419,6 +425,8 @@
         start(bulk[2 * sweep + 2])
         build_some(3 * sweep + 2)
         wait(sums)
+        if sweep == 0:
+            start(bulk[5])
         total = jnp.concatenate(
             [col_all[lax.rem(me - o + ns, ns)] for o in range(ns)], axis=0
         )
@@ -603,29 +611,33 @@
     near = alpha + second * grown
     far = second * alpha
 
-    def slot_of(j):
-        return lax.rem(me - j + ns, ns) if static_came else came[j]
-
-    def put(target, source):
-        for j in range(BLOCKS_DEV):
-            k = slot_of(j)
+    turned_rows = obs_in
+
+    def deliver(target, value_of, before=None):
+        for k in range(ns if static_came else BLOCKS_DEV):
+            j = lax.rem(me - k + ns, ns) if static_came else k
+            slot = k if static_came else came[k]
+            if before is not None:
+                before(k)
             for pair in range(pairs):
-                value = source[k, pair]
-                for parity in range(2):
-                    at = (2 * pair + parity) * cols
-                    target[:, j, at : at + cols] = value[parity * fields : (parity + 1) * fields]
+                at = pl.multiple_of((j * pairs + pair) * lanes, lanes)
+                turned_rows[pl.ds(at, lanes)] = value_of(slot, pair).T
+        for f in range(fields):
+            for r in range(strip_rows):
+                line = (r // 2) * lanes + (r % 2) * fields + f
+                target[f, :, r * cols : (r + 1) * cols] = turned_rows[
+                    pl.ds(line, BLOCKS_DEV, stride=pairs * lanes), :
+                ]
 
     wait(q_exchange)
-    for k in range(ns):
-        for pair in range(pairs):
-            staged_q[k, pair] = (near * recv_p[k, pair] - far * recv_q[k, pair]).T
-            recv_p[k, pair] = recv_p[k, pair] - near * recv_q[k, pair]
-    put(out, staged_q)
-    for k in range(ns):
-        wait(w_copies[k : k + 1])
-        for pair in range(pairs):
-            recv_w[k, pair] = (recv_p[k, pair] + far * recv_w[k, pair]).T
-    put(rest, recv_w)
+    deliver(out, lambda k, pair: near * recv_p[k, pair] - far * recv_q[k, pair])
+    if not static_came:
+        wait(w_copies)
+    deliver(
+        rest,
+        lambda k, pair: (recv_p[k, pair] - near * recv_q[k, pair]) + far * recv_w[k, pair],
+        (lambda k: wait(w_copies[k : k + 1])) if static_came else None,
+    )
 
 
 def owned_table(group_map, owners, per_owner):

time: 118 us -> 115 us (0.975)
  Pallas kernels: 115 us -> 111 us
    pallas_call x1, Pallas kernels: 115 us -> 111 us  [on_device(): pl.pallas_call(functools.partial(solve_kernel, nw, ns, fields, strip_rows...]
where the time goes in v4:
time: 115 us; the launch traced here: 114 us
  Pallas kernels  111 us (97%)
  local copies, waits for them, and re-layouts  1.94 us (2%)
    pallas_call x1, Pallas kernels, on_device(): pl.pallas_call(functools.partial(solve_kernel, nw, ns, fields, strip_rows...  111 us

profile of v4, /device:TPU:10, one launch (start us, length us, event | category | flops | bytes accessed | tf_op | source)
XLA Modules:
  0.0 113.8 jit_solution(11074011799049864453)
XLA Ops:
  0.6 111.3 %shard_map.77 = (f32[64,8,512]{2,1,0:T(8,128)S(1)}, f32[64,8,512]{2,1,0:T(8,128)S(1)}) custom-call(s32[1,64]{1,0:T(1,128)} %owner_hbm.1, s32[1,64]{1,0:T(1,128)} %owner_hbm.1, s32[6,1,64]{2,1,0:T(1,128)} %bitcast.8, f32[2048,128]{1,0:T(8,128)} %bitcast.7, f32[1,64]{1,0:T(1,128)} %bitcast.9, s32[32,128]{1,0:T(8,128)} %seen_hbm.1, f32[2,32,128]{2,1,0:T(8,128)} %jitter_hbm.1), custom_call_target="tpu_custom_call" | custom-call | tf_op jit(solution)/shard_map/pallas_call | solution.py:689
  111.9 1.0 copy.10
  112.9 1.0 copy.11

commit v5 on v4

--- a/solution.py
+++ b/solution.py
@@ -70,11 +70,11 @@
     ]
 
 
-def gathered_sum(buffer, axis, n):
+def gathered_sum(buffer, axis, n, count=None):
     me = lax.axis_index(axis)
     total = None
     for owner in range(n):
-        term = buffer[lax.rem(me - owner + n, n)]
+        term = buffer[lax.rem(me - owner + n, n), 0 : buffer.shape[1] if count is None else count]
         total = term if total is None else total + term
     return total
 
@@ -301,8 +301,13 @@
         centred(row_reach + row_dev, row_reach)
         lines(oth, 0, oth.shape[2])
 
-    def tile_builder(source, first_block, members):
+    def tile_builder(source, first_block, members, together):
         def build(t, carry):
+            for step in range(together):
+                build_one(t * together + step)
+            return carry
+
+        def build_one(t):
             block, i = t // groups, lax.rem(t, groups)
             at = pl.multiple_of(i * GROUP, GROUP)
             first = pl.multiple_of(block * strip_rows, strip_rows)
@@ -333,12 +338,12 @@
                     low = (kernel - high.astype(F32)).astype(jnp.bfloat16)
                     tiles[block, i, parts * n + part, 0:tile_rows] = high
                     tiles[block, i, parts * n + part, tile_rows : 2 * tile_rows] = low
-            return carry
 
         return build
 
-    build_own = tile_builder(own_oth, 0, (0,))
-    build_tile = tile_builder(oth, REACH, tuple(range(1, NEIGHBOURS + 1)))
+    own_together = 4
+    build_own = tile_builder(own_oth, 0, (0,), own_together)
+    build_tile = tile_builder(oth, REACH, tuple(range(1, NEIGHBOURS + 1)), 1)
 
     steps = BLOCKS_DEV * groups
     shares = (0, 9, 19, 29, 42, 53, 64)
@@ -369,7 +374,7 @@
         start(sums)
         if sweep == 0:
             prepare_own()
-            lax.fori_loop(0, steps, build_own, 0)
+            lax.fori_loop(0, steps // own_together, build_own, 0)
             wait(place_copies)
             prepare_all()
         build_some(3 * sweep)
@@ -402,11 +407,13 @@
         for k in range(ns):
             owner_of = lax.rem(me + k, ns)
             col_send[k, 0:chunk] = col_part[pl.ds(pl.multiple_of(owner_of * chunk, chunk), chunk)]
-            col_send[k, chunk : chunk + 8] = jnp.broadcast_to(count, (8, cols))
-        col_got[0] = col_send[0]
+            if sweep == 0:
+                col_send[k, chunk : chunk + 1] = count
+        sent = chunk + 1 if sweep == 0 else chunk
+        col_got[0, 0:sent] = col_send[0, 0:sent]
         sums = [
             remote(
-                col_send.at[k], col_got.at[k],
+                col_send.at[k, pl.ds(0, sent)], col_got.at[k, pl.ds(0, sent)],
                 sem_s.at[2 + sweep, k], sem_r.at[2 + sweep, k], "sixteen", ns, k,
             )
             for k in range(1, ns)
@@ -415,7 +422,7 @@
         start(bulk[2 * sweep + 1])
         build_some(3 * sweep + 1)
         wait(sums)
-        total = gathered_sum(col_got, "sixteen", ns)
+        total = gathered_sum(col_got, "sixteen", ns, sent)
         col_all[0] = total[:chunk]
         if sweep == 0:
             counts = jnp.broadcast_to(total[chunk : chunk + 1], full).T
@@ -649,6 +656,15 @@
     ) * member[:, :, None]
     numbers = jnp.arange(total_strips, dtype=jnp.int32)
     return jnp.sum(slot_hit * numbers[None, :, None], axis=1, dtype=jnp.int32)
+
+
+def hand_over_kernel(first_in, second_in, first_out, second_out, sem):
+    copies = [
+        pltpu.make_async_copy(first_in, first_out, sem.at[0]),
+        pltpu.make_async_copy(second_in, second_out, sem.at[1]),
+    ]
+    start(copies)
+    wait(copies)
 
 
 def on_device(observations, huber_scale, observed, jitter, owner_map, neighbours):
@@ -740,6 +756,17 @@
         observed,
         jitter,
     )
+    if static_came:
+        solution_now, residual_now = pl.pallas_call(
+            hand_over_kernel,
+            out_shape=(out_shape, out_shape),
+            in_specs=[VMEM] * 2,
+            out_specs=(anywhere, anywhere),
+            scratch_shapes=[pltpu.SemaphoreType.DMA((2,))],
+        )(
+            pltpu.with_memory_space_constraint(solution_now, pltpu.VMEM),
+            pltpu.with_memory_space_constraint(residual_now, pltpu.VMEM),
+        )
     return solution_now[None, None], residual_now[None, None]
 
 

time: 115 us -> 113 us (0.983)
  local copies, waits for them, and re-layouts: 1.94 us -> 0 us
    unnamed x2 -> x0, local copies, waits for them, and re-layouts: 1.94 us -> none
    pallas_call x0 -> x1, Pallas kernels: none -> 1.33 us  [on_device(): pl.pallas_call(hand_over_kernel, out_shape=(out_shape, out_shape), in_spe...]
    pallas_call x1, Pallas kernels: 111 us -> 110 us  [on_device(): pl.pallas_call(functools.partial(solve_kernel, nw, ns, fields, strip_rows...]
where the time goes in v5:
time: 113 us; the launch traced here: 112 us
  Pallas kernels  111 us (98%)
    pallas_call x1, Pallas kernels, on_device(): pl.pallas_call(functools.partial(solve_kernel, nw, ns, fields, strip_rows...  110 us

profile of v5, /device:TPU:10, one launch (start us, length us, event | category | flops | bytes accessed | tf_op | source)
XLA Modules:
  0.0 112.0 jit_solution(7398544183259833543)
XLA Ops:
  0.6 110.1 %shard_map.77 = (f32[64,8,512]{2,1,0:T(8,128)S(1)}, f32[64,8,512]{2,1,0:T(8,128)S(1)}) custom-call(s32[1,64]{1,0:T(1,128)} %owner_hbm.1, s32[1,64]{1,0:T(1,128)} %owner_hbm.1, s32[6,1,64]{2,1,0:T(1,128)} %bitcast.6, f32[2048,128]{1,0:T(8,128)} %bitcast.5, f32[1,64]{1,0:T(1,128)} %bitcast.7, s32[32,128]{1,0:T(8,128)} %seen_hbm.1, f32[2,32,128]{2,1,0:T(8,128)} %jitter_hbm.1), custom_call_target="tpu_custom_call" | custom-call | tf_op jit(solution)/shard_map/pallas_call | solution.py:705
  110.7 1.3 %shard_map.78 = (f32[64,8,512]{2,1,0:T(8,128)}, f32[64,8,512]{2,1,0:T(8,128)}) custom-call(f32[64,8,512]{2,1,0:T(8,128)S(1)} %get-tuple-element.6.first_in, f32[64,8,512]{2,1,0:T(8,128)S(1)} %get-tuple-element.7.second_in), custom_call_target="tpu_custom_call" | custom-call | tf_op jit(solution)/shard_map/pallas_call | solution.py:760

commit v6 on v5

--- a/solution.py
+++ b/solution.py
@@ -346,7 +346,7 @@
     build_tile = tile_builder(oth, REACH, tuple(range(1, NEIGHBOURS + 1)), 1)
 
     steps = BLOCKS_DEV * groups
-    shares = (0, 9, 19, 29, 42, 53, 64)
+    shares = (0, 8, 19, 30, 42, 53, 64)
 
     def build_some(part):
         lax.fori_loop(shares[part] * steps // 64, shares[part + 1] * steps // 64, build_tile, 0)

time: 113 us -> 113 us (level)
  no operation moved by 1% of the time
where the time goes in v6:
time: 113 us; the launch traced here: 112 us
  Pallas kernels  112 us (99%)
    pallas_call x1, Pallas kernels, on_device(): pl.pallas_call(functools.partial(solve_kernel, nw, ns, fields, strip_rows...  110 us

profile of v6, /device:TPU:10, one launch (start us, length us, event | category | flops | bytes accessed | tf_op | source)
XLA Modules:
  0.0 112.3 jit_solution(4326426045090912150)
XLA Ops:
  0.6 110.3 %shard_map.77 = (f32[64,8,512]{2,1,0:T(8,128)S(1)}, f32[64,8,512]{2,1,0:T(8,128)S(1)}) custom-call(s32[1,64]{1,0:T(1,128)} %owner_hbm.1, s32[1,64]{1,0:T(1,128)} %owner_hbm.1, s32[6,1,64]{2,1,0:T(1,128)} %bitcast.6, f32[2048,128]{1,0:T(8,128)} %bitcast.5, f32[1,64]{1,0:T(1,128)} %bitcast.7, s32[32,128]{1,0:T(8,128)} %seen_hbm.1, f32[2,32,128]{2,1,0:T(8,128)} %jitter_hbm.1), custom_call_target="tpu_custom_call" | custom-call | tf_op jit(solution)/shard_map/pallas_call | solution.py:705
  111.0 1.3 %shard_map.78 = (f32[64,8,512]{2,1,0:T(8,128)}, f32[64,8,512]{2,1,0:T(8,128)}) custom-call(f32[64,8,512]{2,1,0:T(8,128)S(1)} %get-tuple-element.6.first_in, f32[64,8,512]{2,1,0:T(8,128)S(1)} %get-tuple-element.7.second_in), custom_call_target="tpu_custom_call" | custom-call | tf_op jit(solution)/shard_map/pallas_call | solution.py:760
